TPU v7x, 32 devices: a whole 2x2x4 slice. The times are simulated.
32 devices in a mesh: dp: 8 (over z, y), tensor: 4 (over x, core).
Axes of the slice: x: 2, y: 2, z: 4, core: 2. Of those that a mesh axis runs over, the one named last changes fastest.
Arguments:
- embeddings: bfloat16 [16384, 768], P('dp'), may hold values from -6 to 6
- cotangent: bfloat16 [16384, 768], P('dp'), may hold values from -6 to 6
- species: int32 [8], P('dp'), may hold values from 0 to 2, as said below
- gene_ids: int32 [8, 2048], P('dp'), may hold values from 0 to 32767, as said below
- w_qkv: float32 [3, 768, 768], P(None, 'dp', 'tensor'), may hold values from -0.21875 to 0.21875
- w_out: float32 [768, 768], P('tensor', 'dp'), may hold values from -6 to 6
- w_up: float32 [768, 3072], P('dp', 'tensor'), may hold values from -0.21875 to 0.21875
- w_down: float32 [3072, 768], P('tensor', 'dp'), may hold values from -0.109375 to 0.109375
- norm_gains: float32 [2, 768], P(None, 'dp'), may hold values from 0.1 to 1.9
- norm_shifts: float32 [2, 768], P(None, 'dp'), may hold values from -1.8 to 1.8
Outputs:
- mixed: bfloat16 [16384, 768], P('dp')
- grad_input: bfloat16 [16384, 768], P('dp')
- grad_qkv: float32 [3, 768, 768], P(None, 'dp', 'tensor')
- grad_out: float32 [768, 768], P('tensor', 'dp')
- grad_up: float32 [768, 3072], P('dp', 'tensor')
- grad_down: float32 [3072, 768], P('tensor', 'dp')
- grad_gains: float32 [2, 768], P(None, 'dp')
- grad_shifts: float32 [2, 768], P(None, 'dp')
- grad_ffn_shift: float32 [768], P('dp')
Inputs may be any that keep to these rules, and one draw needn't show every extreme that they name: `species`: 0 marks a human cell, 1 a mouse cell, 2 a padding cell; some cell is a padding cell. `gene_ids`: each cell holds gene ids 1 to 32767 in its first positions and 0 (padding) after them; a cell has 1024 to 2048 nonzero ids, and some cell has 2048.
All inputs are finite; a program needn't handle non-finite values.
Results may differ from a plain program's by a relative error of at most 0.017.
Values may be sent and summed in bfloat16 or wider, within the bound.
No kernel may reach another device: no remote copies, remote signals or barrier semaphores. Data moves between devices by JAX's collectives and lax.ppermute only.
A program may use at most 128 MiB of HBM per device.

v0:
```python
from functools import partial
import math

import jax
import jax.numpy as jnp
from jax import lax
from jax.sharding import PartitionSpec as P

HD = 64


EPSILON = 1e-05
NEGATIVE = -1e30


def layer_norm(inputs, gain, shift):
    center = inputs - jnp.mean(inputs, axis=-1, keepdims=True)
    variance = jnp.mean(center * center, axis=-1, keepdims=True)
    return center * lax.rsqrt(variance + EPSILON) * gain + shift


def attend_block(query_block, key_rows, value_rows, keep, scale):
    raw_scores = (
        jnp.einsum("qhe,khe->hqk", query_block, key_rows, preferred_element_type=jnp.float32)
        * scale
    )
    scores = jnp.where(keep[None, None, :], raw_scores, NEGATIVE)
    highest = jnp.max(scores, axis=-1, keepdims=True)
    shifted = jnp.exp(scores - highest)
    totals = jnp.sum(shifted, axis=-1, keepdims=True)
    weights = (shifted / totals).astype(jnp.bfloat16)
    output = jnp.einsum("hqk,khe->qhe", weights, value_rows, preferred_element_type=jnp.float32)
    return (output, highest + jnp.log(totals))


def attend_cell(element, scale):
    queries, key_rows, value_rows, keep = element
    length, heads_here, head_width = queries.shape
    blocksz = min(512, length)
    blocks = queries.reshape(length // blocksz, blocksz, heads_here, head_width)
    outputs, log_sums = lax.map(
        lambda query_block: attend_block(query_block, key_rows, value_rows, keep, scale), blocks
    )
    return (outputs.reshape(length, heads_here, head_width), log_sums)


def attend_back(element, scale):
    queries, key_rows, value_rows, keep, grad_out, log_sums = element
    length, heads_here, head_width = queries.shape
    blocksz = min(512, length)
    query_blocks = queries.reshape(length // blocksz, blocksz, heads_here, head_width)
    grad_blocks = grad_out.reshape(length // blocksz, blocksz, heads_here, head_width)

    def visit(carry, piece):
        grad_keys, grad_values = carry
        query_block, grad_block, log_block = piece
        raw_scores = (
            jnp.einsum("qhe,khe->hqk", query_block, key_rows, preferred_element_type=jnp.float32)
            * scale
        )
        scores = jnp.where(keep[None, None, :], raw_scores, NEGATIVE)
        probs = jnp.exp(scores - log_block)
        grad_values = grad_values + jnp.einsum(
            "hqk,qhe->khe",
            probs.astype(jnp.bfloat16),
            grad_block,
            preferred_element_type=jnp.float32,
        )
        grad_probs = jnp.einsum(
            "qhe,khe->hqk", grad_block, value_rows, preferred_element_type=jnp.float32
        )
        centre = jnp.sum(probs * grad_probs, axis=-1, keepdims=True)
        grad_scores = (probs * (grad_probs - centre)).astype(jnp.bfloat16)
        grad_query = (
            jnp.einsum("hqk,khe->qhe", grad_scores, key_rows, preferred_element_type=jnp.float32)
            * scale
        )
        grad_keys = (
            grad_keys
            + jnp.einsum(
                "hqk,qhe->khe", grad_scores, query_block, preferred_element_type=jnp.float32
            )
            * scale
        )
        return ((grad_keys, grad_values), grad_query)

    zeros = jnp.zeros(key_rows.shape, jnp.float32)
    (grad_keys, grad_values), grad_queries = lax.scan(
        visit, (zeros, zeros), (query_blocks, grad_blocks, log_sums)
    )
    return (grad_queries.reshape(length, heads_here, head_width), grad_keys, grad_values)


def body(
    embeddings, cotangent, species, gene_ids, w_qkv, w_out, w_up, w_down, norm_gains, norm_shifts
):
    bfloat = jnp.bfloat16
    single = jnp.float32
    cells, genes = gene_ids.shape
    tok_rows, width = embeddings.shape
    scale = 1.0 / math.sqrt(HD)
    query_w, out_w, up_w, down_w, gains_b, shifts_b = (
        lax.all_gather(w_qkv.astype(bfloat), "dp", axis=1, tiled=True),
        lax.all_gather(w_out.astype(bfloat), "dp", axis=1, tiled=True),
        lax.all_gather(w_up.astype(bfloat), "dp", axis=0, tiled=True),
        lax.all_gather(w_down.astype(bfloat), "dp", axis=1, tiled=True),
        lax.all_gather(norm_gains.astype(bfloat), "dp", axis=1, tiled=True),
        lax.all_gather(norm_shifts.astype(bfloat), "dp", axis=1, tiled=True),
    )
    gains = gains_b.astype(single)
    shifts = shifts_b.astype(single)
    local = query_w.shape[2]
    heads_here = local // HD
    keep = gene_ids != 0
    live = jnp.logical_and(keep, (species != 2)[:, None]).reshape(tok_rows, 1).astype(single)
    inputs = embeddings.astype(single)
    normed = layer_norm(inputs, gains[0], shifts[0]).astype(bfloat)
    projected = jnp.einsum("td,cdf->ctf", normed, query_w, preferred_element_type=single).astype(
        bfloat
    )
    queries = projected[0].reshape(cells, genes, heads_here, HD)
    key_rows = projected[1].reshape(cells, genes, heads_here, HD)
    value_rows = projected[2].reshape(cells, genes, heads_here, HD)
    heads_out, log_sums = lax.map(
        partial(attend_cell, scale=scale), (queries, key_rows, value_rows, keep)
    )
    heads_flat = heads_out.reshape(tok_rows, local).astype(bfloat)
    attn_part = jnp.dot(heads_flat, out_w, preferred_element_type=single).astype(bfloat)
    hidden = inputs + lax.psum(attn_part, "tensor").astype(jnp.float32)
    second = layer_norm(hidden, gains[1], shifts[1]).astype(bfloat)
    before = jnp.dot(second, up_w, preferred_element_type=single)
    activated, gelu_back = jax.vjp(partial(jax.nn.gelu, approximate=False), before)
    activated_b = activated.astype(bfloat)
    ffn_part = jnp.dot(activated_b, down_w, preferred_element_type=single).astype(bfloat)
    mixed = (hidden + lax.psum(ffn_part, "tensor").astype(jnp.float32)).astype(bfloat)
    query_w, out_w, up_w, down_w, gains_b, shifts_b = (
        lax.all_gather(w_qkv.astype(bfloat), "dp", axis=1, tiled=True),
        lax.all_gather(w_out.astype(bfloat), "dp", axis=1, tiled=True),
        lax.all_gather(w_up.astype(bfloat), "dp", axis=0, tiled=True),
        lax.all_gather(w_down.astype(bfloat), "dp", axis=1, tiled=True),
        lax.all_gather(norm_gains.astype(bfloat), "dp", axis=1, tiled=True),
        lax.all_gather(norm_shifts.astype(bfloat), "dp", axis=1, tiled=True),
    )
    gains = gains_b.astype(single)
    shifts = shifts_b.astype(single)
    seed_rows = cotangent.astype(single) * live
    seed_b = seed_rows.astype(bfloat)
    grad_down = jnp.einsum("tf,td->fd", activated_b, seed_b, preferred_element_type=single)
    grad_act = jnp.einsum("td,fd->tf", seed_b, down_w, preferred_element_type=single)
    grad_before = gelu_back(grad_act)[0].astype(bfloat)
    grad_up = jnp.einsum("td,tf->df", second, grad_before, preferred_element_type=single)
    grad_second = lax.psum(
        jnp.einsum("tf,df->td", grad_before, up_w, preferred_element_type=single).astype(
            jnp.bfloat16
        ),
        "tensor",
    ).astype(jnp.float32)
    second_fn, second_back = jax.vjp(layer_norm, hidden, gains[1], shifts[1])
    grad_hidden_ln, grad_gain_two, grad_shift_two = second_back(grad_second)
    grad_hidden = seed_rows + grad_hidden_ln
    grad_hidden_b = grad_hidden.astype(bfloat)
    grad_out = jnp.einsum("tf,td->fd", heads_flat, grad_hidden_b, preferred_element_type=single)
    grad_heads = jnp.einsum(
        "td,fd->tf", grad_hidden_b, out_w, preferred_element_type=single
    ).astype(bfloat)
    grad_heads = grad_heads.reshape(cells, genes, heads_here, HD)
    grad_q, grad_k, grad_v = lax.map(
        partial(attend_back, scale=scale),
        (queries, key_rows, value_rows, keep, grad_heads, log_sums),
    )
    grad_proj = jnp.stack(
        [
            grad_q.reshape(tok_rows, local),
            grad_k.reshape(tok_rows, local),
            grad_v.reshape(tok_rows, local),
        ]
    ).astype(bfloat)
    grad_qkv = jnp.einsum("td,ctf->cdf", normed, grad_proj, preferred_element_type=single)
    grad_normed = lax.psum(
        jnp.einsum("ctf,cdf->td", grad_proj, query_w, preferred_element_type=single).astype(
            jnp.bfloat16
        ),
        "tensor",
    ).astype(jnp.float32)
    first_fn, first_back = jax.vjp(layer_norm, inputs, gains[0], shifts[0])
    grad_inputs_ln, grad_gain_one, grad_shift_one = first_back(grad_normed)
    grad_input = (grad_hidden + grad_inputs_ln).astype(bfloat)
    gain_grads = jnp.stack([grad_gain_one, grad_gain_two])
    shift_grads = jnp.stack([grad_shift_one, grad_shift_two])
    sent_qkv, sent_out, sent_up, sent_down, sent_gains, sent_shifts = (
        lax.psum_scatter(grad_qkv, "dp", scatter_dimension=1, tiled=True),
        lax.psum_scatter(grad_out, "dp", scatter_dimension=1, tiled=True),
        lax.psum_scatter(grad_up, "dp", scatter_dimension=0, tiled=True),
        lax.psum_scatter(grad_down, "dp", scatter_dimension=1, tiled=True),
        lax.psum_scatter(gain_grads, "dp", scatter_dimension=1, tiled=True),
        lax.psum_scatter(shift_grads, "dp", scatter_dimension=1, tiled=True),
    )
    return (
        mixed,
        grad_input,
        sent_qkv,
        sent_out,
        sent_up,
        sent_down,
        sent_gains,
        sent_shifts,
        sent_shifts[1],
    )


def solution(mesh):
    return jax.shard_map(
        body,
        mesh=mesh,
        in_specs=(
            P("dp", None),
            P("dp", None),
            P("dp"),
            P("dp", None),
            P(None, "dp", "tensor"),
            P("tensor", "dp"),
            P("dp", "tensor"),
            P("tensor", "dp"),
            P(None, "dp"),
            P(None, "dp"),
        ),
        out_specs=(
            P("dp", None),
            P("dp", None),
            P(None, "dp", "tensor"),
            P("tensor", "dp"),
            P("dp", "tensor"),
            P("tensor", "dp"),
            P(None, "dp"),
            P(None, "dp"),
            P("dp"),
        ),
        check_vma=False,
    )
```

profile of v0, /device:TPU:0, one launch (start us, length us, event | category | flops | bytes accessed | tf_op | source)
XLA Modules:
  0.0 984.3 jit_solution(3351383576825054261)
XLA Ops:
  10.4 22.9 %all-gather.1 = bf16[8,96,2]{1,2,0:T(2,128)(2,1)} all-gather(bf16[1,96,2]{1,2,0:T(2,128)(2,1)S(1)} %convert_bitcast_fusion.1), channel_id=1, replica_groups=mesh['dp'=8,'tensor'=4] {'dp'}, dimensions={0}, use_global_device_ids=true | all-gather | bytes 3456 | tf_op jit(solution)/shard_map/all_gather | solution.py:108
  33.3 16.1 %all-gather = bf16[8,96,2]{1,2,0:T(2,128)(2,1)S(1)} all-gather(bf16[1,96,2]{1,2,0:T(2,128)(2,1)S(1)} %convert_bitcast_fusion.2), channel_id=1, replica_groups=mesh['dp'=8,'tensor'=4] {'dp'}, dimensions={0}, use_global_device_ids=true | all-gather | bytes 3456 | tf_op jit(solution)/shard_map/all_gather | solution.py:107
  58.3 31.5 %all_gather.26 = bf16[192,768]{0,1:T(8,128)(2,1)S(1)} all-gather(bf16[192,96]{0,1:T(8,128)(2,1)} %copy.54), channel_id=1, replica_groups=mesh['dp'=8,'tensor'=4] {'dp'}, dimensions={1}, use_global_device_ids=true | all-gather | bytes 331776 | tf_op jit(solution)/shard_map/all_gather | solution.py:104
  89.8 36.7 %all_gather.25 = bf16[3,768,192]{2,0,1:T(4,128)(2,1)} all-gather(bf16[3,96,192]{2,0,1:T(4,128)(2,1)S(1)} %copy.50), channel_id=1, replica_groups=mesh['dp'=8,'tensor'=4] {'dp'}, dimensions={1}, use_global_device_ids=true | all-gather | bytes 995328 | tf_op jit(solution)/shard_map/all_gather | solution.py:103
  142.0 42.6 %while.47 = (s32[]{:T(128)}, bf16[4,512,3,64]{1,3,2,0:T(8,128)(2,1)}, f32[4,3,512,1]{2,1,3,0:T(4,128)}, pred[2048]{0:T(1024)(128)(4,1)S(1)}, bf16[4,512,3,64]{1,...) while((s32[]{:T(128)}, bf16[4,512,3,64]{1,3,2,0:T(8,128)(2,1)}, ...), condition=%wide.region_5.6_spmd, body=%wide.region_2.5_spmd.sunk | while | flops 843053568 | bytes 49410236 | solution.py:41
  193.9 63.5 %all-reduce.5.cloned.1.call-done = bf16[2048,768]{1,0:T(8,128)(2,1)} async-done(((bf16[2048,768]{1,0:T(8,128)(2,1)}), bf16[2048,768]{1,0:T(8,128)(2,1)}) %all-reduce.5.cloned.1.call-update) | async-done | bytes 3145744 | tf_op jit(solution)/shard_map/psum | solution.py:129
  266.5 18.7 %multiply_convert_fusion.1 = (bf16[2048,768]{1,0:T(8,128)(2,1)}, f32[2048,768]{1,0:T(8,128)}, f32[2048,768]{1,0:T(8,128)}) fusion(bf16[2048,768]{1,0:T(8,128)(2,1)} %add_convert_fusion.3, bf16[768,768]{1,0:T(8,128)(2,1)} %all-gather.5.cloned.1.call-done), kind=kOutput, calls=%fused_computation.81 | convolution fusion | flops 2518155264 | bytes 20054016 | tf_op jit(solution)/shard_map/dot_general | solution.py:131
  285.2 8.2 add_convert_fusion.1
  299.6 6.5 convolution_convert_fusion.1
  306.1 61.7 %all-reduce.7.cloned.1.call-done = bf16[2048,768]{1,0:T(8,128)(2,1)} async-done(((bf16[2048,768]{1,0:T(8,128)(2,1)}), bf16[2048,768]{1,0:T(8,128)(2,1)}) %all-reduce.7.cloned.1.call-update) | async-done | bytes 3145744 | tf_op jit(solution)/shard_map/psum | solution.py:152
  367.8 5.9 fusion.55
  389.6 107.4 %while.48 = (s32[]{:T(128)}, f32[2048,3,64]{0,2,1:T(8,128)S(1)}, f32[2048,3,64]{0,2,1:T(8,128)}, bf16[4,512,3,64]{1,3,2,0:T(8,128)(2,1)}, bf16[4,512,3,64]{1,3,2...) while((s32[]{:T(128)}, f32[2048,3,64]{0,2,1:T(8,128)S(1)}, ...), condition=%wide.region_15.16_spmd.clone, body=%wide.region_13.15_spmd.clone.sunk | while | flops 2062514688 | bytes 129417400 | solution.py:88
  408.1 5.7 fusion.149
  435.0 5.6 fusion.149
  461.9 5.6 fusion.149
  514.2 114.6 %all-reduce.9.cloned.1.call-done = (bf16[2048,768]{1,0:T(8,128)(2,1)}, bf16[2048,768]{1,0:T(8,128)(2,1)}) async-done(((bf16[2048,768]{1,0:T(8,128)(2,1)}, bf16[2048,768]{1,0:T(8,128)(2,1)}), (bf16[2048,768]{1,0:T(8,128)(2,1)}, bf16[2048,768]{1,0:T(8,128)(2,1)})) %all-reduce.9.cloned.1.call-update) | async-done | bytes 6291472 | tf_op jit(solution)/shard_map/psum | solution.py:135
  652.8 6.9 fusion.88
  659.8 7.0 fusion.72
  668.6 11.4 %add_convert_fusion = (bf16[2048,768]{1,0:T(8,128)(2,1)}, bf16[2048,768]{1,0:T(8,128)(2,1)}) fusion(bf16[2048,768]{1,0:T(8,128)(2,1)S(1)} %copy-done.2, bf16[2048,768]{1,0:T(8,128)(2,1)} %get-tuple-element.340, f32[2048,768]{1,0:T(8,128)} %copy-done.7, bf16[2048,768]{1,0:T(8,128)(2,1)} %param.15, f32[2048]{0:T(1024)S(1)} %negate_multiply_fusion.1, ...), kind=kLoop, calls=%fused_computation.75 | loop fusion | flops 31457280 | bytes 28363776 | tf_op jit(solution)/shard_map/convert_element_type | solution.py:187
  679.9 19.2 %reduce-scatter.23.cloned.1.call-done = f32[96,2]{1,0:T(8,128)} async-done(((f32[768,2]{1,0:T(8,128)}), f32[96,2]{1,0:T(8,128)}) %reduce-scatter.23.cloned.1.call-update) | async-done | bytes 784
  700.6 62.7 %reduce-scatter.25.cloned.1.call-done = f32[96,2]{1,0:T(8,128)} async-done(((f32[768,2]{1,0:T(8,128)}), f32[96,2]{1,0:T(8,128)}) %reduce-scatter.25.cloned.1.call-update) | async-done | bytes 784
  764.7 68.4 %reduce-scatter.19.cloned.1.call-done = f32[96,576]{1,0:T(8,128)} async-done(((f32[768,576]{1,0:T(8,128)}), f32[96,576]{1,0:T(8,128)}) %reduce-scatter.19.cloned.1.call-update) | async-done | bytes 221200
  834.9 69.9 %reduce-scatter.15.cloned.1.call-done = f32[96,768]{1,0:T(8,128)} async-done(((f32[768,768]{1,0:T(8,128)}), f32[96,768]{1,0:T(8,128)}) %reduce-scatter.15.cloned.1.call-update) | async-done | bytes 294928 | tf_op jit(solution)/shard_map/reduce_scatter | solution.py:193
  904.8 72.1 %reduce-scatter.17.cloned.1.call-done = f32[768,96]{0,1:T(8,128)} async-done(((f32[768,768]{0,1:T(8,128)}), f32[768,96]{0,1:T(8,128)}) %reduce-scatter.17.cloned.1.call-update) | async-done | bytes 294928 | tf_op jit(solution)/shard_map/reduce_scatter | solution.py:194
  (252 shorter events, 245.8 us)
Async XLA Ops:
  8.0 122.0 %copy-start.1 = (bf16[2048,768]{1,0:T(8,128)(2,1)S(1)}, bf16[2048,768]{1,0:T(8,128)(2,1)}, u32[]{:S(2)}) copy-start(bf16[2048,768]{1,0:T(8,128)(2,1)} %param.14) | copy-start | bytes 9437188
  8.0 49.4 %copy-start.25 = (f32[192,96]{1,0:T(8,128)S(1)}, f32[192,96]{1,0:T(8,128)}, u32[]{:S(2)}) copy-start(f32[192,96]{1,0:T(8,128)} %param.19) | copy-start | bytes 221188
  8.0 50.2 %copy-start.20 = (f32[3,96,192]{2,1,0:T(8,128)S(1)}, f32[3,96,192]{2,1,0:T(8,128)}, u32[]{:S(2)}) copy-start(f32[3,96,192]{2,1,0:T(8,128)} %param.18) | copy-start | bytes 663556
  8.0 249.3 %all-reduce.5.cloned.1.call-start = ((), (), s32[]{:S(2)}) async-start(), calls=%async_computation.6 | async-start | bytes 6291456 | tf_op jit(solution)/shard_map/psum | solution.py:129
  53.9 79.5 %copy-start.21 = (f32[2048]{0:T(1024)}, f32[2048]{0:T(1024)S(1)}, u32[]{:S(2)}) copy-start(f32[2048]{0:T(1024)S(1)} %broadcast_multiply_fusion.1) | copy-start | bytes 24580
  57.5 75.9 %copy-start.32 = (f32[2048]{0:T(1024)}, f32[2048]{0:T(1024)S(1)}, u32[]{:S(2)}) copy-start(f32[2048]{0:T(1024)S(1)} %fusion.78) | copy-start | bytes 24580
  190.1 76.4 %all-gather.5.cloned.1.call-start = ((), (), s32[]{:S(2)}) async-start(), calls=%async_computation.7 | async-start | bytes 1327104 | tf_op jit(solution)/shard_map/all_gather | solution.py:105
  191.9 93.4 %all-gather.7.cloned.1.call-start = ((), (), s32[]{:S(2)}) async-start(), calls=%async_computation.8 | async-start | bytes 1327104 | tf_op jit(solution)/shard_map/all_gather | solution.py:106
  193.6 69.5 %copy-start.37 = (f32[768]{0:T(1024)S(1)}, f32[768]{0:T(1024)}, u32[]{:S(2)}) copy-start(f32[768]{0:T(1024)} %get-tuple-element.301) | copy-start | bytes 9220
  193.6 174.2 %all-reduce.7.cloned.1.call-start = ((), (), s32[]{:S(2)}) async-start(), calls=%async_computation.9 | async-start | bytes 6291456 | tf_op jit(solution)/shard_map/psum | solution.py:152
  285.2 9.8 copy-start.43
  299.1 329.7 %all-reduce.9.cloned.1.call-start = ((), (), s32[]{:S(2)}) async-start(), calls=%async_computation.16 | async-start | bytes 12582912 | tf_op jit(solution)/shard_map/psum | solution.py:135
  508.7 120.1 %copy-start.2 = (bf16[2048,768]{1,0:T(8,128)(2,1)S(1)}, bf16[2048,768]{1,0:T(8,128)(2,1)}, u32[]{:S(2)}) copy-start(bf16[2048,768]{1,0:T(8,128)(2,1)} %param.14) | copy-start | bytes 9437188
  508.7 120.1 %copy-start.22 = (f32[2048]{0:T(1024)S(1)}, f32[2048]{0:T(1024)}, u32[]{:S(2)}) copy-start(f32[2048]{0:T(1024)} %copy-done.21) | copy-start | bytes 24580
  508.7 120.1 %copy-start.36 = (f32[768]{0:T(1024)S(1)}, f32[768]{0:T(1024)}, u32[]{:S(2)}) copy-start(f32[768]{0:T(1024)} %get-tuple-element.302) | copy-start | bytes 9220
  508.7 158.2 %reduce-scatter.21.cloned.1.call-start = ((), (), s32[]{:S(2)}) async-start(), calls=%async_computation.13 | async-start | bytes 884736
  509.4 123.2 %copy-start.27 = (f32[2048]{0:T(1024)S(1)}, f32[2048]{0:T(1024)}, u32[]{:S(2)}) copy-start(f32[2048]{0:T(1024)} %copy-done.26) | copy-start | bytes 24580
  509.4 123.2 %copy-start.33 = (f32[2048]{0:T(1024)S(1)}, f32[2048]{0:T(1024)}, u32[]{:S(2)}) copy-start(f32[2048]{0:T(1024)} %copy-done.32) | copy-start | bytes 24580
  514.1 185.0 %reduce-scatter.23.cloned.1.call-start = ((), (), s32[]{:S(2)}) async-start(), calls=%async_computation.14 | async-start | bytes 442368
  637.3 126.0 %reduce-scatter.25.cloned.1.call-start = ((), (), s32[]{:S(2)}) async-start(), calls=%async_computation.15 | async-start | bytes 442368
  638.3 194.7 %reduce-scatter.19.cloned.1.call-start = ((), (), s32[]{:S(2)}) async-start(), calls=%async_computation.12 | async-start | bytes 2211840
  652.8 252.0 %reduce-scatter.15.cloned.1.call-start = ((), (), s32[]{:S(2)}) async-start(), calls=%async_computation.10 | async-start | bytes 2654208 | tf_op jit(solution)/shard_map/reduce_scatter | solution.py:193
  659.8 317.2 %reduce-scatter.17.cloned.1.call-start = ((), (), s32[]{:S(2)}) async-start(), calls=%async_computation.11 | async-start | bytes 2654208 | tf_op jit(solution)/shard_map/reduce_scatter | solution.py:194
  764.2 212.8 %copy-start.42 = (f32[2,96]{1,0:T(2,128)}, f32[2,96]{1,0:T(2,128)S(1)}, u32[]{:S(2)}) copy-start(f32[2,96]{1,0:T(2,128)S(1)} %copy.67) | copy-start | bytes 2308
  (44 other events, 171.2 us)
Sparse Core Ops, SparseCore 0:
  190.3 67.0 all-reduce.4
  299.2 68.5 all-reduce.6
  508.8 119.8 all-reduce.8
Sparse Core Ops, SparseCore 1:
  193.4 40.0 all-gather.4
  236.0 39.9 all-gather.6
  514.2 62.7 reduce-scatter.20
  637.4 61.7 reduce-scatter.22
  702.8 60.5 reduce-scatter.24
  767.2 65.8 reduce-scatter.18
  837.0 67.8 reduce-scatter.14
  908.7 68.1 reduce-scatter.16
where the time goes:
time: 989 us; the launch traced here: 984 us
  waiting for transfers between devices  532 us (54%)
  matrix products  187 us (19%)
  blocking collectives  107 us (11%)
  other arithmetic  84.5 us (9%)
  local copies, waits for them, and re-layouts  54.7 us (6%)
  between operations  16.9 us (2%)
    unnamed x15, waiting for transfers between devices  150 us
    psum x1, waiting for transfers between devices, body(): lax.psum(ffn_part, 'tensor').astype(jnp.float32)  115 us
    reduce_scatter x1, waiting for transfers between devices, body(): lax.psum_scatter(grad_down, 'dp', scatter_dimension=1, tiled=True)  72.1 us
    reduce_scatter x1, waiting for transfers between devices, body(): lax.psum_scatter(grad_up, 'dp', scatter_dimension=0, tiled=True)  69.9 us
    psum x1, waiting for transfers between devices, body(): hidden = inputs + lax.psum(attn_part, 'tensor').astype(jnp.float32)  63.5 us
    psum x1, waiting for transfers between devices, body(): lax.psum(jnp.einsum('tf,df->td', grad_before, up_w, preferred_element_typ...  61.7 us
    all_gather x1, blocking collectives, body(): lax.all_gather(w_qkv.astype(bfloat), 'dp', axis=1, tiled=True)  36.7 us
    all_gather x1, blocking collectives, body(): lax.all_gather(w_out.astype(bfloat), 'dp', axis=1, tiled=True)  31.5 us
  transfers between devices with their start and end apart: 11, of which 8 were waited for; matrix products, arithmetic and copies ran while one was open for 10% of the time, Pallas kernels for 0%

commit v1 on v0

v1 whole, which is shorter than its diff:
```python
import functools
import math

import jax
import jax.numpy as jnp
from jax import lax
from jax.experimental import pallas as pl
from jax.experimental.pallas import tpu as pltpu
from jax.sharding import PartitionSpec as P

HD = 64
EPSILON = 1e-05
NEGATIVE = -1e30
LOG2E = math.log2(math.e)
bf = jnp.bfloat16
f32 = jnp.float32
NN = ((1,), (0,))
NT = ((1,), (1,))
TN = ((0,), (0,))
ORDER = (0, 2, 1, 3)


def dot(a, b, dims):
    return lax.dot_general(a, b, (dims, ((), ())), preferred_element_type=f32)


def swap(value, axis, mask, size):
    return lax.ppermute(value, axis, [(i, i ^ mask) for i in range(size)])


def split3(v):
    a = v.astype(bf)
    rest = v - a.astype(f32)
    b = rest.astype(bf)
    c = (rest - b.astype(f32)).astype(bf)
    return [a.astype(f32), b.astype(f32), c.astype(f32)]


def with_tail(block, rows):
    q = block.shape[1]
    index = lax.broadcasted_iota(jnp.int32, (HD, q), 0)
    tail = jnp.zeros((HD, q), f32)
    for i, row in enumerate(rows):
        tail = jnp.where(index == i, row, tail)
    return jnp.concatenate([block, tail.astype(bf)], axis=0)


def project_kernel(heads, t_ref, x_ref, w_ref, norm_ref, a_ref, kp_ref, vp_ref, kt_ref, vt_ref, qt_ref, wt_scr, wk_scr, wv_scr):
    step = pl.program_id(0)
    rows = x_ref.shape[0]

    @pl.when(step == 0)
    def _():
        wt_scr[...] = w_ref[...].T
        zero = jnp.zeros((w_ref.shape[0], HD), bf)
        for h in range(heads):
            base = 3 * HD * h
            wk_scr[:, 2 * HD * h : 2 * HD * (h + 1)] = jnp.concatenate([w_ref[:, base + HD : base + 2 * HD], zero], axis=1)
            wv_scr[:, 2 * HD * h : 2 * HD * (h + 1)] = jnp.concatenate([w_ref[:, base + 2 * HD : base + 3 * HD], zero], axis=1)

    x = x_ref[...].astype(f32)
    center = x - jnp.mean(x, axis=-1, keepdims=True)
    variance = jnp.mean(center * center, axis=-1, keepdims=True)
    a = (center * lax.rsqrt(variance + EPSILON) * norm_ref[0:1, :] + norm_ref[2:3, :]).astype(bf)
    a_ref[...] = a
    block = step ^ t_ref[0]
    token = block * rows + lax.broadcasted_iota(jnp.int32, (rows, 2 * HD * heads), 0)
    lane = lax.broadcasted_iota(jnp.int32, (rows, 2 * HD * heads), 1) % (2 * HD)
    ones = jnp.where((lane > HD) & (lane < HD + 4), 1.0, 0.0)
    bias = jnp.where((lane == HD) & (token >= t_ref[1]), NEGATIVE, ones)
    kp_ref[...] = (dot(a, wk_scr[...], NN) + bias).astype(bf)
    vp_ref[...] = (dot(a, wv_scr[...], NN) + ones).astype(bf)
    both = dot(wt_scr[...], a, NT)
    for h in range(heads):
        base = 3 * HD * h
        at = slice(HD * h, HD * (h + 1))
        qt_ref[at, :] = (both[base : base + HD] * 0.125).astype(bf)
        kt_ref[at, :] = both[base + HD : base + 2 * HD].astype(bf)
        vt_ref[at, :] = both[base + 2 * HD : base + 3 * HD].astype(bf)


def project(scalars, x, w, norms):
    count, width = x.shape
    heads = w.shape[1] // (3 * HD)
    rows = count // 4
    block = lambda i, t: (i ^ t[0], 0)
    turned = lambda i, t: (0, i ^ t[0])
    whole = lambda i, t: (0, 0)
    wide = 2 * HD * heads
    spec = pltpu.PrefetchScalarGridSpec(
        num_scalar_prefetch=1,
        grid=(4,),
        in_specs=[
            pl.BlockSpec((rows, width), block),
            pl.BlockSpec(w.shape, whole),
            pl.BlockSpec(norms.shape, whole),
        ],
        out_specs=[
            pl.BlockSpec((rows, width), lambda i, t: (i, 0)),
            pl.BlockSpec((rows, wide), block),
            pl.BlockSpec((rows, wide), block),
            pl.BlockSpec((HD * heads, rows), turned),
            pl.BlockSpec((HD * heads, rows), turned),
            pl.BlockSpec((HD * heads, rows), turned),
        ],
        scratch_shapes=[
            pltpu.VMEM((w.shape[1], width), bf),
            pltpu.VMEM((width, wide), bf),
            pltpu.VMEM((width, wide), bf),
        ],
    )
    return pl.pallas_call(
        functools.partial(project_kernel, heads),
        grid_spec=spec,
        out_shape=[
            jax.ShapeDtypeStruct((count, width), bf),
            jax.ShapeDtypeStruct((count, wide), bf),
            jax.ShapeDtypeStruct((count, wide), bf),
            jax.ShapeDtypeStruct((HD * heads, count), bf),
            jax.ShapeDtypeStruct((HD * heads, count), bf),
            jax.ShapeDtypeStruct((HD * heads, count), bf),
        ],
        compiler_params=pltpu.CompilerParams(vmem_limit_bytes=48 << 20),
        cost_estimate=pl.CostEstimate(flops=2 * count * width * 5 * HD * heads, bytes_accessed=count * width * 8, transcendentals=0),
        name="project",
    )(scalars, x, w, norms)


def attend_kernel(chunk, t_ref, kp_ref, vt_ref, qt_ref, o_ref, lse_ref, s_scr):
    q = qt_ref.shape[1]
    keys = kp_ref.shape[0]
    queries = with_tail(qt_ref[...], [jnp.ones((1, q), f32)])
    top = None
    for i in range(keys // chunk):
        at = slice(i * chunk, (i + 1) * chunk)
        s = dot(kp_ref[at, :], queries, NN)
        s_scr[at, :] = s
        here = jnp.max(s, axis=0, keepdims=True)
        top = here if top is None else jnp.maximum(top, here)
    total = None
    out = None
    for i in range(keys // chunk):
        at = slice(i * chunk, (i + 1) * chunk)
        p = jnp.exp2((s_scr[at, :] - top) * LOG2E)
        here = jnp.sum(p, axis=0, keepdims=True)
        part = dot(vt_ref[:, at], p.astype(bf), NN)
        total = here if total is None else total + here
        out = part if out is None else out + part
    o_ref[0] = (out / total).astype(bf)
    lse_ref[0, 0] = jnp.broadcast_to(top + jnp.log(total), (8, q))


def attend(scalars, kp, vt, qt):
    count = kp.shape[0]
    heads = qt.shape[0] // HD
    q = count // 4
    spec = pltpu.PrefetchScalarGridSpec(
        num_scalar_prefetch=1,
        grid=(heads, 4),
        in_specs=[
            pl.BlockSpec((count, 2 * HD), lambda h, i, t: (0, h)),
            pl.BlockSpec((HD, count), lambda h, i, t: (h, 0)),
            pl.BlockSpec((HD, q), lambda h, i, t: (h, i ^ t[0])),
        ],
        out_specs=[
            pl.BlockSpec((1, HD, q), lambda h, i, t: (i, h, 0)),
            pl.BlockSpec((1, 1, 8, q), lambda h, i, t: (h, i, 0, 0)),
        ],
        scratch_shapes=[pltpu.VMEM((count, q), f32)],
    )
    return pl.pallas_call(
        functools.partial(attend_kernel, min(512, count)),
        grid_spec=spec,
        out_shape=[
            jax.ShapeDtypeStruct((4, heads * HD, q), bf),
            jax.ShapeDtypeStruct((heads, 4, 8, q), f32),
        ],
        compiler_params=pltpu.CompilerParams(vmem_limit_bytes=48 << 20),
        cost_estimate=pl.CostEstimate(flops=heads * 4 * count * count * 256, bytes_accessed=heads * count * 512, transcendentals=heads * count * count),
        name="attend",
    )(scalars, kp, vt, qt)


def attend_back_kernel(chunk, t_ref, kp_ref, vp_ref, kt_ref, qt_ref, o_ref, lse_ref, do_ref, out_ref, dk_scr, dv_scr):
    q = qt_ref.shape[1]
    keys = kp_ref.shape[0]
    step = pl.program_id(0)

    @pl.when(step == 0)
    def _():
        dk_scr[...] = jnp.zeros_like(dk_scr)
        dv_scr[...] = jnp.zeros_like(dv_scr)

    qt = qt_ref[...]
    do = do_ref[0]
    delta = jnp.sum(do.astype(f32) * o_ref[0].astype(f32), axis=0, keepdims=True)
    one = jnp.ones((1, q), f32)
    queries = with_tail(qt, [one] + [-v for v in split3(lse_ref[0, 0, 0:1])])
    grads = with_tail(do, [0.0 * one] + [-v for v in split3(delta)])
    dq = None
    for i in range(keys // chunk):
        at = slice(i * chunk, (i + 1) * chunk)
        p = jnp.exp2(dot(kp_ref[at, :], queries, NN) * LOG2E)
        dp = dot(vp_ref[at, :], grads, NN)
        ds = (p * dp).astype(bf)
        dv_scr[at, :] += dot(p.astype(bf), do, NT)
        dk_scr[at, :] += dot(ds, qt, NT)
        part = dot(kt_ref[:, at], ds, NN)
        dq = part if dq is None else dq + part
    out_ref[step, 0:HD, :] = (dq * 0.125).astype(bf)

    @pl.when(step == pl.num_programs(0) - 1)
    def _():
        for i in range(4):
            at = pl.ds(pl.multiple_of((i ^ t_ref[0]) * q, q), q)
            out_ref[i, HD : 2 * HD, :] = dk_scr[at, :].T.astype(bf)
            out_ref[i, 2 * HD : 3 * HD, :] = dv_scr[at, :].T.astype(bf)


def attend_back(scalars, kp, vp, kt, qt, o, lse, do, h):
    count = kp.shape[0]
    q = count // 4
    whole = lambda i, t: (0, h)
    spec = pltpu.PrefetchScalarGridSpec(
        num_scalar_prefetch=1,
        grid=(4,),
        in_specs=[
            pl.BlockSpec((count, 2 * HD), whole),
            pl.BlockSpec((count, 2 * HD), whole),
            pl.BlockSpec((HD, count), lambda i, t: (h, 0)),
            pl.BlockSpec((HD, q), lambda i, t: (h, i ^ t[0])),
            pl.BlockSpec((1, HD, q), lambda i, t: (i, h, 0)),
            pl.BlockSpec((1, 1, 8, q), lambda i, t: (h, i, 0, 0)),
            pl.BlockSpec((1, HD, q), lambda i, t: (i, h, 0)),
        ],
        out_specs=pl.BlockSpec((4, 3 * HD, q), lambda i, t: (0, 0, 0)),
        scratch_shapes=[pltpu.VMEM((count, HD), f32), pltpu.VMEM((count, HD), f32)],
    )
    return pl.pallas_call(
        functools.partial(attend_back_kernel, min(512, count)),
        grid_spec=spec,
        out_shape=jax.ShapeDtypeStruct((4, 3 * HD, q), bf),
        compiler_params=pltpu.CompilerParams(vmem_limit_bytes=48 << 20),
        cost_estimate=pl.CostEstimate(flops=10 * count * count * 256, bytes_accessed=count * 2048, transcendentals=count * count),
        name=f"attend_back{h}",
    )(scalars, kp, vp, kt, qt, o, lse, do)


def place(pieces, index, size):
    out = jnp.zeros((size,) + pieces[0].shape, pieces[0].dtype)
    for s, piece in enumerate(pieces):
        out = lax.dynamic_update_slice(out, piece[None], (index ^ s,) + (0,) * piece.ndim)
    return out


def gather_rows(piece, n):
    if n != 8:
        return lax.all_gather(piece, "dp", axis=0)
    d = lax.axis_index("dp")
    along_z = place([piece] + [swap(piece, "dp", 2 * s, n) for s in (1, 2, 3)], d // 2, 4)
    other = swap(along_z, "dp", 1, n)
    both = jnp.where(d % 2 == 0, jnp.stack([along_z, other], 1), jnp.stack([other, along_z], 1))
    return both.reshape((n,) + piece.shape)


def gather_all(piece, n):
    pair = jnp.stack([piece, swap(piece, "tensor", 2, 4)])
    rows = gather_rows(pair, n)
    mine = jnp.moveaxis(rows, 1, 0)
    return jnp.concatenate([mine, swap(mine, "tensor", 1, 4)])


def scatter_rows(value, n):
    if n != 8:
        return lax.psum_scatter(value, "dp", scatter_dimension=0, tiled=False).astype(f32)
    d = lax.axis_index("dp")
    pairs = value.reshape((4, 2) + value.shape[1:])
    keep = lax.dynamic_index_in_dim(pairs, d % 2, 1, False)
    send = lax.dynamic_index_in_dim(pairs, 1 - d % 2, 1, False)
    half = (keep.astype(f32) + swap(send, "dp", 1, n).astype(f32)).astype(bf)
    z = d // 2
    total = lax.dynamic_index_in_dim(half, z, 0, False).astype(f32)
    for s in (1, 2, 3):
        total = total + swap(lax.dynamic_index_in_dim(half, z ^ s, 0, False), "dp", 2 * s, n).astype(f32)
    return total


def scatter_all(mine, theirs, n):
    pair = (mine.astype(f32) + swap(theirs, "tensor", 1, 4).astype(f32)).astype(bf)
    one = (pair[0].astype(f32) + swap(pair[1], "tensor", 2, 4).astype(f32)).astype(bf)
    return scatter_rows(one, n)


def collect(block):
    t = lax.axis_index("tensor")
    across = swap(block, "tensor", 2, 4)
    pieces = [block, swap(block, "tensor", 1, 4), across, swap(across, "tensor", 1, 4)]
    return place(pieces, t, 4).reshape(4 * block.shape[0], block.shape[1])


def exchange(blocks):
    return [blocks[0]] + [swap(blocks[k], "tensor", k, 4) for k in (1, 2, 3)]


def sum_everywhere(value, n):
    value = value + swap(value, "tensor", 1, 4)
    value = value + swap(value, "tensor", 2, 4)
    if n != 8:
        return lax.psum(value, "dp")
    value = value + swap(value, "dp", 1, n)
    return value + swap(value, "dp", 2, n) + swap(value, "dp", 4, n) + swap(value, "dp", 6, n)


def normalize(v):
    center = v - jnp.mean(v, axis=-1, keepdims=True)
    variance = jnp.mean(center * center, axis=-1, keepdims=True)
    r = lax.rsqrt(variance + EPSILON)
    return center * r, r


def norm_back(dn, n, r, gain):
    scaled = dn * gain
    return r * (scaled - jnp.mean(scaled, axis=-1, keepdims=True) - n * jnp.mean(scaled * n, axis=-1, keepdims=True))


def body(n, embeddings, cotangent, species, gene_ids, w_qkv, w_out, w_up, w_down, norm_gains, norm_shifts):
    t = lax.axis_index("tensor")
    d = lax.axis_index("dp")
    count, width = embeddings.shape
    rows = count // 4
    r = width // n
    local = w_qkv.shape[2]
    heads = local // HD
    units = w_up.shape[1]
    length = jnp.sum((gene_ids != 0).astype(jnp.int32))
    alive = jnp.where(species[0] == 2, 0, length)
    scalars = jnp.stack([t.astype(jnp.int32), length])

    qkv_own = w_qkv.astype(bf).reshape(3, r, heads, HD).transpose(1, 2, 0, 3).reshape(r, 3 * local)
    norms_own = jnp.concatenate([norm_gains, norm_shifts]).astype(bf)
    norms_own = jnp.pad(norms_own, ((0, 12), (0, 3 * local - r)))
    first = gather_rows(jnp.concatenate([qkv_own, norms_own]), n)
    w_first = first[:, :r].reshape(width, 3 * local)
    norms = first[:, r : r + 4, :r].transpose(1, 0, 2).reshape(4, width).astype(f32)
    rest_own = jnp.concatenate([w_out.astype(bf).T, w_up.astype(bf), w_down.astype(bf).T], axis=1)
    rest = gather_all(rest_own, n).reshape(4, width, local + 2 * units)
    out_t, up, down_t = rest[:, :, :local], rest[:, :, local : local + units], rest[:, :, local + units :]
    pair = jnp.stack([w_first, swap(w_first, "tensor", 2, 4)])
    w_all = jnp.concatenate([pair, swap(pair, "tensor", 1, 4)])

    normed, kp, vp, kt, vt, qt = project(scalars, embeddings, w_first, norms)
    o_local, lse = attend(scalars, kp, vt, qt)
    o_here = exchange(o_local)
    o = jnp.stack([o_here[k] for k in ORDER])

    start = t * rows
    x = lax.dynamic_slice(embeddings, (start, 0), (rows, width)).astype(f32)
    g = lax.dynamic_slice(cotangent, (start, 0), (rows, width)).astype(f32)
    g = jnp.where(start + lax.broadcasted_iota(jnp.int32, (rows, 1), 0) < alive, g, 0.0)
    gb = g.astype(bf)
    h = x + jnp.einsum("kft,kdf->td", o, out_t, preferred_element_type=f32)
    n2, r2 = normalize(h)
    c = (n2 * norms[1:2] + norms[3:4]).astype(bf)
    u = jnp.einsum("td,kdu->ktu", c, up, preferred_element_type=f32)
    phi = 0.5 * (1.0 + lax.erf(u * math.sqrt(0.5)))
    e = (u * phi).astype(bf)
    de = jnp.einsum("td,kdu->ktu", gb, down_t, preferred_element_type=f32)
    du = (de * (phi + u * jnp.exp(-0.5 * u * u) * (1.0 / math.sqrt(2.0 * math.pi)))).astype(bf)
    dc = jnp.einsum("ktu,kdu->td", du, up, preferred_element_type=f32)
    dh = g + norm_back(dc, n2, r2, norms[1:2])
    dhb = dh.astype(bf)
    do = jnp.einsum("kdf,td->kft", out_t, dhb, preferred_element_type=f32).astype(bf)
    do_back = exchange([do[ORDER.index(k)] for k in range(4)])
    do_local = jnp.stack(do_back)
    mixed = collect((h + jnp.einsum("ktu,kdu->td", e, down_t, preferred_element_type=f32)).astype(bf))

    g_out = jnp.einsum("td,kft->kdf", dhb, o, preferred_element_type=f32).astype(bf)
    g_up = jnp.einsum("td,ktu->kdu", c, du, preferred_element_type=f32).astype(bf)
    g_down = jnp.einsum("td,ktu->kdu", gb, e, preferred_element_type=f32).astype(bf)
    cut = lambda v: v.reshape(2, n, r, v.shape[-1])
    s_down = scatter_all(cut(g_down[:2]), cut(g_down[2:]), n)
    s_up = scatter_all(cut(g_up[:2]), cut(g_up[2:]), n)
    s_out = scatter_all(cut(g_out[:2]), cut(g_out[2:]), n)

    parts, arrived = [], []
    for head in range(heads):
        grads = attend_back(scalars, kp, vp, kt, qt, o_local, lse, do_local, head)
        parts.append(grads)
        arrived.append(exchange(grads))
    normed = normed.reshape(4, rows, width)
    g_first = jnp.concatenate([jnp.einsum("ktd,kft->df", normed, p, preferred_element_type=f32).astype(bf) for p in parts], axis=1)
    s_first = scatter_rows(g_first.reshape(n, r, 3 * local), n)
    dqkv = jnp.stack([jnp.concatenate([a[k] for a in arrived], axis=0) for k in ORDER])
    da = jnp.einsum("kft,kdf->td", dqkv, w_all, preferred_element_type=f32)
    n1, r1 = normalize(x)
    dx = dh + norm_back(da, n1, r1, norms[0:1])
    grad_input = collect(dx.astype(bf))
    sums = jnp.stack([jnp.sum(da * n1, 0), jnp.sum(dc * n2, 0), jnp.sum(da, 0), jnp.sum(dc, 0)])
    sums = lax.dynamic_slice(sum_everywhere(sums, n), (0, d * r), (4, r))
    s_qkv = s_first.reshape(r, heads, 3, HD).transpose(2, 0, 1, 3).reshape(3, r, local)
    return (mixed, grad_input, s_qkv, s_out.T, s_up, s_down.T, sums[:2], sums[2:], sums[3])


def solution(mesh):
    return jax.shard_map(
        functools.partial(body, mesh.shape["dp"]),
        mesh=mesh,
        in_specs=(
            P("dp", None),
            P("dp", None),
            P("dp"),
            P("dp", None),
            P(None, "dp", "tensor"),
            P("tensor", "dp"),
            P("dp", "tensor"),
            P("tensor", "dp"),
            P(None, "dp"),
            P(None, "dp"),
        ),
        out_specs=(
            P("dp", None),
            P("dp", None),
            P(None, "dp", "tensor"),
            P("tensor", "dp"),
            P("dp", "tensor"),
            P("tensor", "dp"),
            P(None, "dp"),
            P(None, "dp"),
            P("dp"),
        ),
        check_vma=False,
    )
```

time: 989 us -> 537 us (0.54)
  waiting for transfers between devices: 532 us -> 241 us
  matrix products: 187 us -> 46.3 us
  blocking collectives: 107 us -> 0 us
  starting transfers between devices: 1.09 us -> 81.8 us
  Pallas kernels: 0 us -> 71 us
  other arithmetic: 84.5 us -> 37 us
  between operations: 16.9 us -> 3.34 us
    ppermute x0 -> x61, waiting for transfers between devices: none -> 241 us  [swap(): return lax.ppermute(value, axis, [(i, i ^ mask) for i in range(size)])]
    psum x3 -> x0, waiting for transfers between devices: 240 us -> none  [the longest x1 115 us: body(): lax.psum(ffn_part, 'tensor').astype(jnp.float32)]
    unnamed x15 -> x0, waiting for transfers between devices: 150 us -> none
    reduce_scatter x2 -> x0, waiting for transfers between devices: 142 us -> none  [the longest x1 72.1 us: body(): lax.psum_scatter(grad_down, 'dp', scatter_dimension=1, tiled=True)]
    dot_general x38 -> x13, matrix products: 179 us -> 46.3 us  [the longest x1 6.76 us: body(): u = jnp.einsum('td,kdu->ktu', c, up, preferred_element_type=f32)]
    all_gather x4 -> x0, blocking collectives: 107 us -> none  [the longest x1 36.7 us: body(): lax.all_gather(w_qkv.astype(bfloat), 'dp', axis=1, tiled=True)]
    ppermute x0 -> x61, starting transfers between devices: none -> 81.8 us  [swap(): return lax.ppermute(value, axis, [(i, i ^ mask) for i in range(size)])]
    pallas_call x0 -> x5, Pallas kernels: none -> 71 us  [the longest x3 38.6 us: attend_back(): pl.pallas_call(functools.partial(attend_back_kernel, min(512, count)), gr...]
  transfers between devices with their start and end apart: 11 -> 61, of which waited for: 8 -> 31; matrix products, arithmetic and copies ran while one was open for 10% -> 21% of each run, Pallas kernels for 0% -> 13%
where the time goes in v1:
time: 537 us; the launch traced here: 529 us
  waiting for transfers between devices  241 us (45%)
  starting transfers between devices  81.8 us (15%)
  Pallas kernels  71 us (13%)
  local copies, waits for them, and re-layouts  48.5 us (9%)
  matrix products  46.3 us (9%)
  other arithmetic  37 us (7%)
    ppermute x61, waiting for transfers between devices, swap(): return lax.ppermute(value, axis, [(i, i ^ mask) for i in range(size)])  241 us
    ppermute x61, starting transfers between devices, swap(): return lax.ppermute(value, axis, [(i, i ^ mask) for i in range(size)])  81.8 us
    pallas_call x3, Pallas kernels, attend_back(): pl.pallas_call(functools.partial(attend_back_kernel, min(512, count)), gr...  38.6 us
    pallas_call x1, Pallas kernels, attend(): pl.pallas_call(functools.partial(attend_kernel, min(512, count)), grid_sp...  22.5 us
    unnamed x72, local copies, waits for them, and re-layouts  11.3 us
  transfers between devices with their start and end apart: 61, of which 31 were waited for; matrix products, arithmetic and copies ran while one was open for 21% of the time, Pallas kernels for 13%

profile of v1, /device:TPU:0, one launch (start us, length us, event | category | flops | bytes accessed | tf_op | source)
XLA Modules:
  0.0 529.0 jit_solution(8345062715311722286)
XLA Ops:
  6.9 8.1 %collective-permute-done.7 = bf16[96,1728]{1,0:T(8,128)(2,1)S(1)} collective-permute-done((bf16[96,1728]{1,0:T(8,128)(2,1)S(1)}, bf16[96,1728]{1,0:T(8,128)(2,1)S(1)}, u32[]{:S(2)}, u32[]{:S(2)}) %collective-permute-start.7) | collective-permute-done | bytes 331808 | tf_op jit(solution)/shard_map/ppermute | solution.py:28
  20.5 25.8 %collective-permute-done.8 = bf16[2,96,1728]{2,1,0:T(8,128)(2,1)} collective-permute-done((bf16[2,96,1728]{2,1,0:T(8,128)(2,1)}, bf16[2,96,1728]{2,1,0:T(8,128)(2,1)}, u32[]{:S(2)}, u32[]{:S(2)}) %collective-permute-start.8) | collective-permute-done | bytes 663584 | tf_op jit(solution)/shard_map/ppermute | solution.py:28
  47.5 19.2 %collective-permute-done.9 = bf16[2,96,1728]{2,1,0:T(8,128)(2,1)S(1)} collective-permute-done((bf16[2,96,1728]{2,1,0:T(8,128)(2,1)}, bf16[2,96,1728]{2,1,0:T(8,128)(2,1)S(1)}, u32[]{:S(2)}, u32[]{:S(2)}) %collective-permute-start.9) | collective-permute-done | bytes 663584 | tf_op jit(solution)/shard_map/ppermute | solution.py:28
  68.4 55.7 %collective-permute-done.11 = bf16[4,2,96,1728]{3,2,1,0:T(8,128)(2,1)} collective-permute-done((bf16[4,2,96,1728]{3,2,1,0:T(8,128)(2,1)S(1)}, bf16[4,2,96,1728]{3,2,1,0:T(8,128)(2,1)}, u32[]{:S(2)}, u32[]{:S(2)}) %collective-permute-start.11) | collective-permute-done | bytes 2654240 | tf_op jit(solution)/shard_map/ppermute | solution.py:28
  131.0 15.3 %collective-permute-start = (bf16[112,576]{0,1:T(8,128)(2,1)S(1)}, bf16[112,576]{0,1:T(8,128)(2,1)S(1)}, u32[]{:S(2)}, u32[]{:S(2)}) collective-permute-start(bf16[112,576]{0,1:T(8,128)(2,1)S(1)} %fusion.83), channel_id=1, source_target_pairs={{0,8},{4,12},{8,0},{12,4},{16,24},{20,28},{24,16},{28,20},{1,9},{5... | collective-permute-start | bytes 387080 | tf_op jit(solution)/shard_map/ppermute | solution.py:28
  153.7 6.5 %collective-permute-done.1 = bf16[112,576]{0,1:T(8,128)(2,1)S(1)} collective-permute-done((bf16[112,576]{0,1:T(8,128)(2,1)S(1)}, bf16[112,576]{0,1:T(8,128)(2,1)S(1)}, u32[]{:S(2)}, u32[]{:S(2)}) %collective-permute-start.1) | collective-permute-done | bytes 129056 | tf_op jit(solution)/shard_map/ppermute | solution.py:28
  165.6 8.7 %collective-permute-done.3 = bf16[4,112,576]{2,1,0:T(8,128)(2,1)S(1)} collective-permute-done((bf16[4,112,576]{2,1,0:T(8,128)(2,1)S(1)}, bf16[4,112,576]{2,1,0:T(8,128)(2,1)S(1)}, u32[]{:S(2)}, u32[]{:S(2)}) %collective-permute-start.3) | collective-permute-done | bytes 516128 | tf_op jit(solution)/shard_map/ppermute | solution.py:28
  177.6 9.9 %project.1 = (bf16[2048,768]{1,0:T(8,128)(2,1)}, bf16[2048,384]{1,0:T(8,128)(2,1)S(1)}, bf16[2048,384]{1,0:T(8,128)(2,1)}, bf16[192,2048]{1,0:T(8,128)(2,1)S(1)}...) custom-call(s32[2]{0:T(128)S(1)} %pad_add_fusion.t_ref, bf16[2048,768]{1,0:T(8,128)(2,1)} %x_ref.1, ...), custom_call_target="tpu_custom_call" | custom-call | flops 3019898880 | bytes 12582912 | tf_op jit(solution)/shard_map/project/pallas_call | solution.py:112
  187.6 22.5 %attend.1 = (bf16[4,192,512]{2,1,0:T(8,128)(2,1)S(1)}, f32[3,4,8,512]{3,2,1,0:T(8,128)S(1)}) custom-call(s32[2]{0:T(128)S(1)} %pad_add_fusion.t_ref, bf16[2048,384]{1,0:T(8,128)(2,1)S(1)} %get-tuple-element.17.kp_ref, bf16[192,2048]{1,0:T(8,128)(2,1)S(1)} %get-tuple-element.18.vt_ref, bf16[192,2048]{1,0:T(8,128)(2,1)S(1)} %get-tuple-element.19.qt_ref), custom_call_target="tpu_custom_call" | custom-call | flops 12884901888 | bytes 3145728 | tf_op jit(solution)/shard_map/attend/pallas_call | solution.py:171
  220.5 5.7 %pad_maximum_fusion = bf16[4,8,96,1728]{3,2,0,1:T(8,128)(2,1)S(1)} fusion(bf16[2,8,96,1728]{3,2,0,1:T(8,128)(2,1)} %collective-permute-done.12, bf16[2,8,96,1728]{3,2,0,1:T(8,128)(2,1)} %bitcast.31), kind=kLoop, calls=%fused_computation | loop fusion | flops 5308416 | bytes 21233664 | tf_op jit(solution)/shard_map/concatenate | solution.py:270
  231.4 6.8 %fusion.9 = (bf16[4,512,768]{1,2,0:T(8,128)(2,1)}, f32[4,768,512]{2,1,0:T(8,128)S(1)}) fusion(f32[512,768]{1,0:T(8,128)S(1)} %get-tuple-element.115, f32[768]{0:T(1024)S(1)} %copy-done.27, f32[768]{0:T(1024)S(1)} %copy-done.24, f32[512]{0:T(512)S(1)} %add_rsqrt_fusion.1, f32[512]{0:T(512)S(1)} %broadcast_multiply_fusion.5, ...), kind=kOutput, calls=%fused_computation.13 | convolution fusion | flops 2425749504 | bytes 15740928 | tf_op jit(solution)/shard_map/td,kdu->ktu/dot_general | solution.py:364
  238.1 6.7 %fusion.5 = bf16[4,512,768]{1,2,0:T(8,128)(2,1)S(1)} fusion(f32[4,768,512]{2,1,0:T(8,128)S(1)} %get-tuple-element.119, bf16[4,768,1728]{2,1,0:T(8,128)(2,1)S(1)} %bitcast.307, pred[512]{0:T(512)(128)(4,1)S(1)} %copy-done.28, bf16[2048,768]{1,0:T(8,128)(2,1)S(1)} %copy-done.20, s32[]{:T(128)S(6)} %select_n.139), kind=kOutput, calls=%fused_computation.7 | convolution fusion | flops 2432827392 | bytes 14942724 | tf_op jit(solution)/shard_map/td,kdu->ktu/dot_general | solution.py:367
  246.5 5.0 fusion.49
  263.0 5.1 convert_bitcast_fusion
  274.9 5.4 %bitcast_dynamic-update-slice_fusion.7 = (bf16[4,512,768]{2,1,0:T(8,128)(2,1)S(1)}, bf16[512,768]{1,0:T(8,128)(2,1)}) fusion(bf16[4,512,768]{2,1,0:T(8,128)(2,1)S(1)} %broadcast.87.clone, s32[]{:T(128)S(6)} %select_n.152, f32[512,768]{1,0:T(8,128)S(1)} %get-tuple-element.115, bf16[4,512,768]{1,2,0:T(8,128)(2,1)S(1)} %copy-done.32, ...), kind=kOutput, calls=%fused_computation.118 | convolution fusion | flops 2416705536 | bytes 11010052 | tf_op jit(solution)/shard_map/ktu,kdu->td/dot_general | solution.py:375
  289.7 12.8 %attend_back0.1 = bf16[4,192,512]{2,1,0:T(8,128)(2,1)S(1)} custom-call(s32[2]{0:T(128)S(1)} %pad_add_fusion.t_ref, bf16[2048,384]{1,0:T(8,128)(2,1)S(1)} %get-tuple-element.17.kp_ref, bf16[2048,384]{1,0:T(8,128)(2,1)} %get-tuple-element.21.vp_ref, bf16[192,2048]{1,0:T(8,128)(2,1)S(1)} %copy-done.1, bf16[192,2048]{1,0:T(8,128)(2,1)S(1)} %copy-done.3, ...), custom_call_target="tpu_custom_call" | custom-call | flops 10737418240 | bytes 4194304 | tf_op jit(solution)/shard_map/attend_back0/pallas_call | solution.py:239
  302.5 12.8 %attend_back1.1 = bf16[4,192,512]{2,1,0:T(8,128)(2,1)S(1)} custom-call(s32[2]{0:T(128)S(1)} %pad_add_fusion.t_ref, bf16[2048,384]{1,0:T(8,128)(2,1)S(1)} %get-tuple-element.17.kp_ref, bf16[2048,384]{1,0:T(8,128)(2,1)} %get-tuple-element.21.vp_ref, bf16[192,2048]{1,0:T(8,128)(2,1)S(1)} %copy-done.1, bf16[192,2048]{1,0:T(8,128)(2,1)S(1)} %copy-done.3, ...), custom_call_target="tpu_custom_call" | custom-call | flops 10737418240 | bytes 4194304 | tf_op jit(solution)/shard_map/attend_back1/pallas_call | solution.py:239
  315.3 13.0 %attend_back2.1 = bf16[4,192,512]{2,1,0:T(8,128)(2,1)S(1)} custom-call(s32[2]{0:T(128)S(1)} %pad_add_fusion.t_ref, bf16[2048,384]{1,0:T(8,128)(2,1)S(1)} %get-tuple-element.17.kp_ref, bf16[2048,384]{1,0:T(8,128)(2,1)} %get-tuple-element.21.vp_ref, bf16[192,2048]{1,0:T(8,128)(2,1)S(1)} %copy-done.1, bf16[192,2048]{1,0:T(8,128)(2,1)S(1)} %copy-done.3, ...), custom_call_target="tpu_custom_call" | custom-call | flops 10737418240 | bytes 4194304 | tf_op jit(solution)/shard_map/attend_back2/pallas_call | solution.py:239
  388.9 8.0 %collective-permute-done.33 = bf16[4,96,576]{2,1,0:T(8,128)(2,1)S(1)} collective-permute-done((bf16[4,96,576]{2,1,0:T(8,128)(2,1)S(1)}, bf16[4,96,576]{2,1,0:T(8,128)(2,1)S(1)}, u32[]{:S(2)}, u32[]{:S(2)}) %collective-permute-start.33) | collective-permute-done | bytes 442400 | tf_op jit(solution)/shard_map/ppermute | solution.py:28
  421.6 7.5 %collective-permute-done.14 = bf16[512,768]{1,0:T(8,128)(2,1)} collective-permute-done((bf16[512,768]{1,0:T(8,128)(2,1)}, bf16[512,768]{1,0:T(8,128)(2,1)}, u32[]{:S(2)}, u32[]{:S(2)}) %collective-permute-start.14) | collective-permute-done | bytes 786464 | tf_op jit(solution)/shard_map/ppermute | solution.py:28
  449.1 20.7 %collective-permute-done.50 = bf16[8,96,768]{2,1,0:T(8,128)(2,1)S(1)} collective-permute-done((bf16[8,96,768]{2,1,0:T(8,128)(2,1)S(1)}, bf16[8,96,768]{2,1,0:T(8,128)(2,1)S(1)}, u32[]{:S(2)}, u32[]{:S(2)}) %collective-permute-start.50) | collective-permute-done | bytes 1179680 | tf_op jit(solution)/shard_map/ppermute | solution.py:28
  471.7 23.0 %collective-permute-done.44 = bf16[8,96,768]{2,1,0:T(8,128)(2,1)S(1)} collective-permute-done((bf16[8,96,768]{2,1,0:T(8,128)(2,1)S(1)}, bf16[8,96,768]{2,1,0:T(8,128)(2,1)S(1)}, u32[]{:S(2)}, u32[]{:S(2)}) %collective-permute-start.44) | collective-permute-done | bytes 1179680 | tf_op jit(solution)/shard_map/ppermute | solution.py:28
  504.0 6.0 %collective-permute-done.45 = bf16[4,96,768]{2,1,0:T(8,128)(2,1)S(1)} collective-permute-done((bf16[4,96,768]{2,1,0:T(8,128)(2,1)S(1)}, bf16[4,96,768]{2,1,0:T(8,128)(2,1)S(1)}, u32[]{:S(2)}, u32[]{:S(2)}) %collective-permute-start.45) | collective-permute-done | bytes 589856 | tf_op jit(solution)/shard_map/ppermute | solution.py:28
  518.8 9.0 %collective-permute-done.47 = bf16[96,768]{1,0:T(8,128)(2,1)S(1)} collective-permute-done((bf16[96,768]{1,0:T(8,128)(2,1)S(1)}, bf16[96,768]{1,0:T(8,128)(2,1)S(1)}, u32[]{:S(2)}, u32[]{:S(2)}) %collective-permute-start.47) | collective-permute-done | bytes 147488 | tf_op jit(solution)/shard_map/ppermute | solution.py:28
  (308 shorter events, 206.5 us)
Async XLA Ops:
  15.8 30.5 %collective-permute-start.8 = (bf16[2,96,1728]{2,1,0:T(8,128)(2,1)}, bf16[2,96,1728]{2,1,0:T(8,128)(2,1)}, u32[]{:S(2)}, u32[]{:S(2)}) collective-permute-start(bf16[2,96,1728]{2,1,0:T(8,128)(2,1)} %pad_maximum_fusion.5), channel_id=1, source_target_pairs={{0,8},{4,12},{8,0},{12,4},{16,24},{20,28},{24,16},{28,20},{1,9},{5... | collective-permute-start | bytes 1990664 | tf_op jit(solution)/shard_map/ppermute | solution.py:28
  17.7 49.0 %collective-permute-start.9 = (bf16[2,96,1728]{2,1,0:T(8,128)(2,1)}, bf16[2,96,1728]{2,1,0:T(8,128)(2,1)S(1)}, u32[]{:S(2)}, u32[]{:S(2)}) collective-permute-start(bf16[2,96,1728]{2,1,0:T(8,128)(2,1)} %pad_maximum_fusion.5), channel_id=1, source_target_pairs={{0,16},{4,20},{8,24},{12,28},{16,0},{20,4},{24,8},{28,12},{1,17},{... | collective-permute-start | bytes 1990664 | tf_op jit(solution)/shard_map/ppermute | solution.py:28
  20.3 46.4 %collective-permute-start.10 = (bf16[2,96,1728]{2,1,0:T(8,128)(2,1)}, bf16[2,96,1728]{2,1,0:T(8,128)(2,1)S(1)}, u32[]{:S(2)}, u32[]{:S(2)}) collective-permute-start(bf16[2,96,1728]{2,1,0:T(8,128)(2,1)} %pad_maximum_fusion.5), channel_id=1, source_target_pairs={{0,24},{4,28},{8,16},{12,20},{16,8},{20,12},{24,0},{28,4},{1,25},{... | collective-permute-start | bytes 1990664 | tf_op jit(solution)/shard_map/ppermute | solution.py:28
  66.8 57.2 %collective-permute-start.11 = (bf16[4,2,96,1728]{3,2,1,0:T(8,128)(2,1)S(1)}, bf16[4,2,96,1728]{3,2,1,0:T(8,128)(2,1)}, u32[]{:S(2)}, u32[]{:S(2)}) collective-permute-start(bf16[4,2,96,1728]{3,2,1,0:T(8,128)(2,1)S(1)} %bitcast_dynamic-update-slice_fusion.8), channel_id=1, source_target_pairs={{0,4},{4,0},{8,12},{12,8},{16,20},{20,16},{24,28},{28,24},{1,5},{5... | collective-permute-start | bytes 7962632 | tf_op jit(solution)/shard_map/ppermute | solution.py:28
  130.5 90.0 %collective-permute-start.12 = (bf16[2,8,96,1728]{3,2,0,1:T(8,128)(2,1)}, bf16[2,8,96,1728]{3,2,0,1:T(8,128)(2,1)}, u32[]{:S(2)}, u32[]{:S(2)}) collective-permute-start(bf16[2,8,96,1728]{3,2,0,1:T(8,128)(2,1)} %bitcast.31), channel_id=1, source_target_pairs={{0,1},{1,0},{2,3},{3,2},{4,5},{5,4},{6,7},{7,6},{8,9},{9,8},{10,11... | collective-permute-start | bytes 15925256 | tf_op jit(solution)/shard_map/ppermute | solution.py:28
  131.0 22.6 %collective-permute-start = (bf16[112,576]{0,1:T(8,128)(2,1)S(1)}, bf16[112,576]{0,1:T(8,128)(2,1)S(1)}, u32[]{:S(2)}, u32[]{:S(2)}) collective-permute-start(bf16[112,576]{0,1:T(8,128)(2,1)S(1)} %fusion.83), channel_id=1, source_target_pairs={{0,8},{4,12},{8,0},{12,4},{16,24},{20,28},{24,16},{28,20},{1,9},{5... | collective-permute-start | bytes 387080 | tf_op jit(solution)/shard_map/ppermute | solution.py:28
  176.1 41.5 %collective-permute-start.28 = (bf16[768,576]{0,1:T(8,128)(2,1)}, bf16[768,576]{0,1:T(8,128)(2,1)}, u32[]{:S(2)}, u32[]{:S(2)}) collective-permute-start(bf16[768,576]{0,1:T(8,128)(2,1)} %copy.146), channel_id=1, source_target_pairs={{0,2},{1,3},{2,0},{3,1},{4,6},{5,7},{6,4},{7,5},{8,10},{9,11},{10,... | collective-permute-start | bytes 2654216 | tf_op jit(solution)/shard_map/ppermute | solution.py:28
  210.9 17.4 %collective-permute-start.4 = (bf16[192,512]{1,0:T(8,128)(2,1)}, bf16[192,512]{1,0:T(8,128)(2,1)}, u32[]{:S(2)}, u32[]{:S(2)}) collective-permute-start(bf16[192,512]{1,0:T(8,128)(2,1)} %get-tuple-element.99), channel_id=1, source_target_pairs={{0,2},{1,3},{2,0},{3,1},{4,6},{5,7},{6,4},{7,5},{8,10},{9,11},{10,... | collective-permute-start | bytes 589832 | tf_op jit(solution)/shard_map/ppermute | solution.py:28
  220.5 141.4 %collective-permute-start.29 = (bf16[2,768,576]{1,2,0:T(8,128)(2,1)}, bf16[2,768,576]{1,2,0:T(8,128)(2,1)}, u32[]{:S(2)}, u32[]{:S(2)}) collective-permute-start(bf16[2,768,576]{1,2,0:T(8,128)(2,1)} %pad_maximum_fusion.1), channel_id=1, source_target_pairs={{0,1},{1,0},{2,3},{3,2},{4,5},{5,4},{6,7},{7,6},{8,9},{9,8},{10,11... | collective-permute-start | bytes 5308424 | tf_op jit(solution)/shard_map/ppermute | solution.py:28
  261.1 26.2 %collective-permute-start.16 = (bf16[192,512]{1,0:T(8,128)(2,1)}, bf16[192,512]{1,0:T(8,128)(2,1)}, u32[]{:S(2)}, u32[]{:S(2)}) collective-permute-start(bf16[192,512]{1,0:T(8,128)(2,1)} %get-tuple-element.95), channel_id=1, source_target_pairs={{0,1},{1,0},{2,3},{3,2},{4,5},{5,4},{6,7},{7,6},{8,9},{9,8},{10,11... | collective-permute-start | bytes 589832 | tf_op jit(solution)/shard_map/ppermute | solution.py:28
  261.6 25.7 %collective-permute-start.17 = (bf16[192,512]{1,0:T(8,128)(2,1)}, bf16[192,512]{1,0:T(8,128)(2,1)}, u32[]{:S(2)}, u32[]{:S(2)}) collective-permute-start(bf16[192,512]{1,0:T(8,128)(2,1)} %get-tuple-element.94), channel_id=1, source_target_pairs={{0,2},{1,3},{2,0},{3,1},{4,6},{5,7},{6,4},{7,5},{8,10},{9,11},{10,... | collective-permute-start | bytes 589832 | tf_op jit(solution)/shard_map/ppermute | solution.py:28
  262.1 25.2 %collective-permute-start.18 = (bf16[192,512]{1,0:T(8,128)(2,1)}, bf16[192,512]{1,0:T(8,128)(2,1)}, u32[]{:S(2)}, u32[]{:S(2)}) collective-permute-start(bf16[192,512]{1,0:T(8,128)(2,1)} %get-tuple-element.93), channel_id=1, source_target_pairs={{0,3},{1,2},{2,1},{3,0},{4,7},{5,6},{6,5},{7,4},{8,11},{9,10},{10,... | collective-permute-start | bytes 589832 | tf_op jit(solution)/shard_map/ppermute | solution.py:28
  349.1 89.4 %collective-permute-start.49 = (bf16[2,8,96,768]{3,2,1,0:T(8,128)(2,1)}, bf16[2,8,96,768]{3,2,1,0:T(8,128)(2,1)}, u32[]{:S(2)}, u32[]{:S(2)}) collective-permute-start(bf16[2,8,96,768]{3,2,1,0:T(8,128)(2,1)} %bitcast.121), channel_id=1, source_target_pairs={{0,1},{1,0},{2,3},{3,2},{4,5},{5,4},{6,7},{7,6},{8,9},{9,8},{10,11... | collective-permute-start | bytes 7077896 | tf_op jit(solution)/shard_map/ppermute | solution.py:28
  353.4 34.5 %collective-permute-start.37 = (bf16[2,8,96,192]{3,2,1,0:T(8,128)(2,1)S(1)}, bf16[2,8,96,192]{3,2,1,0:T(8,128)(2,1)S(1)}, u32[]{:S(2)}, u32[]{:S(2)}) collective-permute-start(bf16[2,8,96,192]{3,2,1,0:T(8,128)(2,1)S(1)} %bitcast.336), channel_id=1, source_target_pairs={{0,1},{1,0},{2,3},{3,2},{4,5},{5,4},{6,7},{7,6},{8,9},{9,8},{10,11... | collective-permute-start | bytes 1769480 | tf_op jit(solution)/shard_map/ppermute | solution.py:28
  382.9 58.7 %collective-permute-start.43 = (bf16[2,8,96,768]{3,2,1,0:T(8,128)(2,1)}, bf16[2,8,96,768]{3,2,1,0:T(8,128)(2,1)}, u32[]{:S(2)}, u32[]{:S(2)}) collective-permute-start(bf16[2,8,96,768]{3,2,1,0:T(8,128)(2,1)} %bitcast.108), channel_id=1, source_target_pairs={{0,1},{1,0},{2,3},{3,2},{4,5},{5,4},{6,7},{7,6},{8,9},{9,8},{10,11... | collective-permute-start | bytes 7077896 | tf_op jit(solution)/shard_map/ppermute | solution.py:28
  383.3 35.5 %collective-permute-start.13 = (bf16[512,768]{1,0:T(8,128)(2,1)}, bf16[512,768]{1,0:T(8,128)(2,1)}, u32[]{:S(2)}, u32[]{:S(2)}) collective-permute-start(bf16[512,768]{1,0:T(8,128)(2,1)} %get-tuple-element.121), channel_id=1, source_target_pairs={{0,1},{1,0},{2,3},{3,2},{4,5},{5,4},{6,7},{7,6},{8,9},{9,8},{10,11... | collective-permute-start | bytes 2359304 | tf_op jit(solution)/shard_map/ppermute | solution.py:28
  409.4 19.7 %collective-permute-start.14 = (bf16[512,768]{1,0:T(8,128)(2,1)}, bf16[512,768]{1,0:T(8,128)(2,1)}, u32[]{:S(2)}, u32[]{:S(2)}) collective-permute-start(bf16[512,768]{1,0:T(8,128)(2,1)} %get-tuple-element.121), channel_id=1, source_target_pairs={{0,2},{1,3},{2,0},{3,1},{4,6},{5,7},{6,4},{7,5},{8,10},{9,11},{10,... | collective-permute-start | bytes 2359304 | tf_op jit(solution)/shard_map/ppermute | solution.py:28
  416.3 22.1 %collective-permute-start.31 = (bf16[512,768]{1,0:T(8,128)(2,1)}, bf16[512,768]{1,0:T(8,128)(2,1)S(1)}, u32[]{:S(2)}, u32[]{:S(2)}) collective-permute-start(bf16[512,768]{1,0:T(8,128)(2,1)} %get-tuple-element.73), channel_id=1, source_target_pairs={{0,2},{1,3},{2,0},{3,1},{4,6},{5,7},{6,4},{7,5},{8,10},{9,11},{10,... | collective-permute-start | bytes 2359304 | tf_op jit(solution)/shard_map/ppermute | solution.py:28
  438.5 58.1 %collective-permute-start.32 = (bf16[512,768]{1,0:T(8,128)(2,1)S(1)}, bf16[512,768]{1,0:T(8,128)(2,1)S(1)}, u32[]{:S(2)}, u32[]{:S(2)}) collective-permute-start(bf16[512,768]{1,0:T(8,128)(2,1)S(1)} %collective-permute-done.31), channel_id=1, source_target_pairs={{0,1},{1,0},{2,3},{3,2},{4,5},{5,4},{6,7},{7,6},{8,9},{9,8},{10,11... | collective-permute-start | bytes 2359304 | tf_op jit(solution)/shard_map/ppermute | solution.py:28
  440.9 28.8 %collective-permute-start.50 = (bf16[8,96,768]{2,1,0:T(8,128)(2,1)S(1)}, bf16[8,96,768]{2,1,0:T(8,128)(2,1)S(1)}, u32[]{:S(2)}, u32[]{:S(2)}) collective-permute-start(bf16[8,96,768]{2,1,0:T(8,128)(2,1)S(1)} %slice_bitcast_fusion), channel_id=1, source_target_pairs={{0,2},{1,3},{2,0},{3,1},{4,6},{5,7},{6,4},{7,5},{8,10},{9,11},{10,... | collective-permute-start | bytes 3538952 | tf_op jit(solution)/shard_map/ppermute | solution.py:28
  445.1 49.5 %collective-permute-start.44 = (bf16[8,96,768]{2,1,0:T(8,128)(2,1)S(1)}, bf16[8,96,768]{2,1,0:T(8,128)(2,1)S(1)}, u32[]{:S(2)}, u32[]{:S(2)}) collective-permute-start(bf16[8,96,768]{2,1,0:T(8,128)(2,1)S(1)} %slice_bitcast_fusion.2), channel_id=1, source_target_pairs={{0,2},{1,3},{2,0},{3,1},{4,6},{5,7},{6,4},{7,5},{8,10},{9,11},{10,... | collective-permute-start | bytes 3538952 | tf_op jit(solution)/shard_map/ppermute | solution.py:28
  470.1 26.6 %collective-permute-start.51 = (bf16[4,96,768]{2,1,0:T(8,128)(2,1)S(1)}, bf16[4,96,768]{2,1,0:T(8,128)(2,1)S(1)}, u32[]{:S(2)}, u32[]{:S(2)}) collective-permute-start(bf16[4,96,768]{2,1,0:T(8,128)(2,1)S(1)} %dynamic-slice_bitcast_fusion), channel_id=1, source_target_pairs={{0,4},{4,0},{8,12},{12,8},{16,20},{20,16},{24,28},{28,24},{1,5},{5... | collective-permute-start | bytes 1769480 | tf_op jit(solution)/shard_map/ppermute | solution.py:28
  496.9 20.4 %collective-permute-start.52 = (bf16[96,768]{1,0:T(8,128)(2,1)S(1)}, bf16[96,768]{1,0:T(8,128)(2,1)S(1)}, u32[]{:S(2)}, u32[]{:S(2)}) collective-permute-start(bf16[96,768]{1,0:T(8,128)(2,1)S(1)} %get-tuple-element.100), channel_id=1, source_target_pairs={{0,8},{4,12},{8,0},{12,4},{16,24},{20,28},{24,16},{28,20},{1,9},{5... | collective-permute-start | bytes 442376 | tf_op jit(solution)/shard_map/ppermute | solution.py:28
  499.0 18.4 %collective-permute-start.53 = (bf16[96,768]{1,0:T(8,128)(2,1)S(1)}, bf16[96,768]{1,0:T(8,128)(2,1)S(1)}, u32[]{:S(2)}, u32[]{:S(2)}) collective-permute-start(bf16[96,768]{1,0:T(8,128)(2,1)S(1)} %get-tuple-element.102), channel_id=1, source_target_pairs={{0,16},{4,20},{8,24},{12,28},{16,0},{20,4},{24,8},{28,12},{1,17},{... | collective-permute-start | bytes 442376 | tf_op jit(solution)/shard_map/ppermute | solution.py:28
  (71 other events, 679.3 us)

commit v2 on v0

v2 whole, which is shorter than its diff:
```python
import functools
import math

import jax
import jax.numpy as jnp
from jax import lax
from jax.experimental import pallas as pl
from jax.experimental.pallas import tpu as pltpu
from jax.sharding import PartitionSpec as P

HD = 64
EPSILON = 1e-05
NEGATIVE = -1e30
LOG2E = math.log2(math.e)
bf = jnp.bfloat16
f32 = jnp.float32
NN = ((1,), (0,))
NT = ((1,), (1,))
ANY = pl.BlockSpec(memory_space=pl.ANY)
SDS = jax.ShapeDtypeStruct


def dot(a, b, dims=NN):
    return lax.dot_general(a, b, (dims, ((), ())), preferred_element_type=f32)


def swap(value, axis, mask, size):
    return lax.ppermute(value, axis, [(i, i ^ mask) for i in range(size)])


def core_swap(value):
    return swap(value, "tensor", 1, 4)


def x_swap(value):
    return swap(value, "tensor", 2, 4)


def after(value, *others):
    return lax.optimization_barrier((value,) + others)[0]


def params(mib=48):
    return pltpu.CompilerParams(vmem_limit_bytes=mib << 20)


def cost(flops, moved, exps=0):
    return pl.CostEstimate(flops=int(flops), bytes_accessed=int(moved), transcendentals=int(exps))


def whole(shape):
    return pl.BlockSpec(shape, lambda *_: (0,) * len(shape))


def row_copies(refs, d, count, dst, columns, sem):
    copies = []
    if len(refs) == 1:
        copies.append(pltpu.make_async_copy(refs[0].at[:, columns], dst, sem))
        return copies
    r = count // 8
    for y, ref in enumerate(refs):
        for s in range(4):
            at = pl.multiple_of((d ^ (2 * s + y)) * r, r)
            copies.append(pltpu.make_async_copy(ref.at[s, 0:r, columns], dst.at[pl.ds(at, r), :], sem))
    return copies


def wait_for(dst, sem):
    pltpu.make_async_copy(dst, dst, sem).wait()


def split3(v):
    a = v.astype(bf)
    rest = v - a.astype(f32)
    b = rest.astype(bf)
    c = (rest - b.astype(f32)).astype(bf)
    return [a.astype(f32), b.astype(f32), c.astype(f32)]


def with_tail(block, rows):
    q = block.shape[1]
    index = lax.broadcasted_iota(jnp.int32, (HD, q), 0)
    tail = jnp.zeros((HD, q), f32)
    for i, row in enumerate(rows):
        tail = jnp.where(index == i, row, tail)
    return jnp.concatenate([block, tail.astype(bf)], axis=0)


def normalize(v):
    center = v - jnp.mean(v, axis=-1, keepdims=True)
    variance = jnp.mean(center * center, axis=-1, keepdims=True)
    r = lax.rsqrt(variance + EPSILON)
    return center * r, r


def norm_back(dn, n, r, gain):
    scaled = dn * gain
    return r * (scaled - jnp.mean(scaled, axis=-1, keepdims=True) - n * jnp.mean(scaled * n, axis=-1, keepdims=True))


def project_kernel(heads, pieces, c_ref, x_ref, *refs):
    w_refs = refs[:pieces]
    n_ref = refs[pieces] if pieces == 1 else None
    a_ref, kp_ref, vp_ref, kt_ref, vt_ref, qt_ref, norm_ref, w_scr, n_scr, wt_scr, wk_scr, wv_scr, sems = refs[pieces + (pieces == 1) :]
    step = pl.program_id(0)
    rows, width = x_ref.shape
    local = HD * heads

    @pl.when(step == 0)
    def _():
        copies = row_copies(w_refs, c_ref[1], width, w_scr, slice(0, 3 * local), sems.at[0])
        if pieces == 1:
            copies.append(pltpu.make_async_copy(n_ref, n_scr.at[0], sems.at[1]))
        else:
            r = width // 8
            for y, ref in enumerate(w_refs):
                for s in range(4):
                    copies.append(pltpu.make_async_copy(ref.at[s, r : r + 16, :], n_scr.at[4 * y + s], sems.at[1]))
        for copy in copies:
            copy.start()
        wait_for(n_scr, sems.at[1])
        found = jnp.sum(n_scr[...].astype(f32), axis=0)
        norm_ref[0:4, :] = jnp.concatenate([found[0:4, 0 : width // 2], found[4:8, 0 : width // 2]], axis=1)
        wait_for(w_scr, sems.at[0])
        wt_scr[...] = w_scr[...].T
        zero = jnp.zeros((width, HD), bf)
        for h in range(heads):
            at = slice(2 * HD * h, 2 * HD * (h + 1))
            wk_scr[:, at] = jnp.concatenate([w_scr[:, local + HD * h : local + HD * (h + 1)], zero], axis=1)
            wv_scr[:, at] = jnp.concatenate([w_scr[:, 2 * local + HD * h : 2 * local + HD * (h + 1)], zero], axis=1)

    n, _ = normalize(x_ref[...].astype(f32))
    a = (n * norm_ref[0:1, :] + norm_ref[2:3, :]).astype(bf)
    a_ref[...] = a
    token = (step ^ c_ref[0]) * rows + lax.broadcasted_iota(jnp.int32, (rows, 2 * local), 0)
    lane = lax.broadcasted_iota(jnp.int32, (rows, 2 * local), 1) % (2 * HD)
    ones = jnp.where((lane > HD) & (lane < HD + 4), 1.0, 0.0)
    bias = jnp.where((lane == HD) & (token >= c_ref[2]), NEGATIVE, ones)
    kp_ref[...] = (dot(a, wk_scr[...]) + bias).astype(bf)
    vp_ref[...] = (dot(a, wv_scr[...]) + ones).astype(bf)
    both = dot(wt_scr[...], a, NT)
    qt_ref[...] = (both[0:local] * 0.125).astype(bf)
    kt_ref[...] = both[local : 2 * local].astype(bf)
    vt_ref[...] = both[2 * local : 3 * local].astype(bf)


def project(scalars, x, w, norms, local):
    count, width = x.shape
    heads = local // HD
    rows = count // 4
    block = lambda i, c: (i ^ c[0], 0)
    turned = lambda i, c: (0, i ^ c[0])
    extra = [] if norms is None else [norms]
    spec = pltpu.PrefetchScalarGridSpec(
        num_scalar_prefetch=1,
        grid=(4,),
        in_specs=[pl.BlockSpec((rows, width), block)] + [ANY] * (len(w) + len(extra)),
        out_specs=[
            pl.BlockSpec((rows, width), lambda i, c: (i, 0)),
            pl.BlockSpec((rows, 2 * local), block),
            pl.BlockSpec((rows, 2 * local), block),
            pl.BlockSpec((local, rows), turned),
            pl.BlockSpec((local, rows), turned),
            pl.BlockSpec((local, rows), turned),
            whole((8, width)),
        ],
        scratch_shapes=[
            pltpu.VMEM((width, 3 * local), bf),
            pltpu.VMEM((8 if len(w) == 2 else 1, 16, 3 * local), bf),
            pltpu.VMEM((3 * local, width), bf),
            pltpu.VMEM((width, 2 * local), bf),
            pltpu.VMEM((width, 2 * local), bf),
            pltpu.SemaphoreType.DMA((2,)),
        ],
    )
    return pl.pallas_call(
        functools.partial(project_kernel, heads, len(w)),
        grid_spec=spec,
        out_shape=[SDS((count, width), bf), SDS((count, 2 * local), bf), SDS((count, 2 * local), bf)]
        + [SDS((local, count), bf)] * 3
        + [SDS((8, width), f32)],
        compiler_params=params(),
        cost_estimate=cost(14 * count * width * local, 24 << 20),
        name="project",
    )(scalars, x, *w, *extra)


def attend_kernel(chunk, c_ref, kp_ref, vt_ref, qt_ref, o_ref, lse_ref, s_scr):
    q = qt_ref.shape[1]
    keys = kp_ref.shape[0]
    queries = with_tail(qt_ref[...], [jnp.ones((1, q), f32)])
    top = None
    for i in range(keys // chunk):
        at = slice(i * chunk, (i + 1) * chunk)
        s = dot(kp_ref[at, :], queries)
        s_scr[at, :] = s
        here = jnp.max(s, axis=0, keepdims=True)
        top = here if top is None else jnp.maximum(top, here)
    total = None
    out = None
    for i in range(keys // chunk):
        at = slice(i * chunk, (i + 1) * chunk)
        p = jnp.exp2((s_scr[at, :] - top) * LOG2E)
        here = jnp.sum(p, axis=0, keepdims=True)
        part = dot(vt_ref[:, at], p.astype(bf))
        total = here if total is None else total + here
        out = part if out is None else out + part
    o_ref[0] = (out / total).astype(bf)
    lse_ref[0, 0] = jnp.broadcast_to(top + jnp.log(total), (8, q))


def attend(scalars, kp, vt, qt, part):
    count = kp.shape[0]
    heads = qt.shape[0] // HD
    q = count // 4
    spec = pltpu.PrefetchScalarGridSpec(
        num_scalar_prefetch=1,
        grid=(heads, 2),
        in_specs=[
            pl.BlockSpec((count, 2 * HD), lambda h, i, c: (0, h)),
            pl.BlockSpec((HD, count), lambda h, i, c: (h, 0)),
            pl.BlockSpec((HD, q), lambda h, i, c: (h, (2 * part + i) ^ c[0])),
        ],
        out_specs=[
            pl.BlockSpec((1, HD, q), lambda h, i, c: (i, h, 0)),
            pl.BlockSpec((1, 1, 8, q), lambda h, i, c: (h, i, 0, 0)),
        ],
        scratch_shapes=[pltpu.VMEM((count, q), f32)],
    )
    return pl.pallas_call(
        functools.partial(attend_kernel, min(512, count)),
        grid_spec=spec,
        out_shape=[SDS((2, heads * HD, q), bf), SDS((heads, 2, 8, q), f32)],
        compiler_params=params(),
        cost_estimate=cost(heads * 2 * count * count * 256, heads * count * 512, heads * count * count // 2),
        name=f"attend{part}",
    )(scalars, kp, vt, qt)


def out_kernel(pieces, c_ref, o_ref, other_ref, *refs):
    mine, theirs, (part_ref, w_scr, sem) = refs[:pieces], refs[pieces : 2 * pieces], refs[2 * pieces :]
    width = part_ref.shape[0]
    for k, group in enumerate((mine, theirs)):
        for copy in row_copies(group, c_ref[1], width, w_scr.at[k], slice(0, 256), sem.at[k]):
            copy.start()
    local = o_ref.shape[1]
    wait_for(w_scr.at[0], sem.at[0])
    part = dot(w_scr[0, :, 0:local], o_ref[0])
    wait_for(w_scr.at[1], sem.at[1])
    part_ref[...] = (part + dot(w_scr[1, :, 0:local], other_ref[...])).astype(bf)


def out_product(scalars, o, other, mine, theirs, width):
    local, q = other.shape
    spec = pltpu.PrefetchScalarGridSpec(
        num_scalar_prefetch=1,
        grid=(1,),
        in_specs=[whole(o.shape), whole(other.shape)] + [ANY] * (2 * len(mine)),
        out_specs=whole((width, q)),
        scratch_shapes=[pltpu.VMEM((2, width, 256), bf), pltpu.SemaphoreType.DMA((2,))],
    )
    return pl.pallas_call(
        functools.partial(out_kernel, len(mine)),
        grid_spec=spec,
        out_shape=SDS((width, q), bf),
        compiler_params=params(),
        cost_estimate=cost(4 * local * width * q, 2 << 20),
        name="out_product",
    )(scalars, o, other, *mine, *theirs)


def ffn_kernel(part, pieces, c_ref, x_ref, g_ref, own_ref, recv_ref, norm_ref, *refs):
    groups = [refs[i * pieces : (i + 1) * pieces] for i in range(4)]
    h_ref, c_out, gb_ref, e_ref, du_ref, ffn_ref, dc_ref, w_scr, sem = refs[4 * pieces :]
    rows, width = x_ref.shape
    units = e_ref.shape[2]
    for j, group in enumerate(groups):
        for copy in row_copies(group, c_ref[1], width, w_scr.at[j], slice(0, units), sem.at[j]):
            copy.start()
    h = x_ref[...].astype(f32) + (own_ref[...].astype(f32) + recv_ref[...].astype(f32)).T
    h_ref[...] = h
    n2, _ = normalize(h)
    c = (n2 * norm_ref[1:2, :] + norm_ref[3:4, :]).astype(bf)
    c_out[...] = c
    token = ((2 * part) ^ c_ref[0]) * rows + lax.broadcasted_iota(jnp.int32, (rows, 1), 0)
    gb = jnp.where(token < c_ref[3], g_ref[...].astype(f32), 0.0).astype(bf)
    gb_ref[...] = gb
    ffn = dc = None
    for k in range(2):
        wait_for(w_scr.at[2 * k], sem.at[2 * k])
        u = dot(c, w_scr[2 * k])
        wait_for(w_scr.at[2 * k + 1], sem.at[2 * k + 1])
        de = dot(gb, w_scr[2 * k + 1])
        phi = 0.5 * (1.0 + lax.erf(u * math.sqrt(0.5)))
        e = (u * phi).astype(bf)
        e_ref[k] = e
        du = (de * (phi + u * jnp.exp(-0.5 * u * u) * (1.0 / math.sqrt(2.0 * math.pi)))).astype(bf)
        du_ref[k] = du
        one, two = dot(du, w_scr[2 * k], NT), dot(e, w_scr[2 * k + 1], NT)
        dc = one if dc is None else dc + one
        ffn = two if ffn is None else ffn + two
    dc_ref[...] = dc.astype(bf)
    ffn_ref[...] = ffn.astype(bf)


def ffn(part, scalars, x, g, own, recv, norms, up, down, up_other, down_other, units):
    width, rows = own.shape
    token_block = pl.BlockSpec((rows, width), lambda i, c: ((2 * part) ^ c[0], 0))
    weights = [*up, *down, *up_other, *down_other]
    spec = pltpu.PrefetchScalarGridSpec(
        num_scalar_prefetch=1,
        grid=(1,),
        in_specs=[token_block, token_block, whole(own.shape), whole(own.shape), whole(norms.shape)] + [ANY] * len(weights),
        out_specs=[whole((rows, width))] * 3 + [whole((2, rows, units))] * 2 + [whole((rows, width))] * 2,
        scratch_shapes=[pltpu.VMEM((4, width, units), bf), pltpu.SemaphoreType.DMA((4,))],
    )
    return pl.pallas_call(
        functools.partial(ffn_kernel, part, len(up)),
        grid_spec=spec,
        out_shape=[SDS((rows, width), f32), SDS((rows, width), bf), SDS((rows, width), bf)]
        + [SDS((2, rows, units), bf)] * 2
        + [SDS((rows, width), bf)] * 2,
        compiler_params=params(),
        cost_estimate=cost(16 * rows * width * units, 16 << 20, 4 * rows * units),
        name=f"ffn{part}",
    )(scalars, x, g, own, recv, norms, *weights)


def middle_kernel(part, pieces, c_ref, h_ref, own_ref, recv_ref, g_ref, norm_ref, *refs):
    mine, theirs = refs[:pieces], refs[pieces : 2 * pieces]
    dh_ref, dhb_ref, do_ref, sum_ref, w_scr, sem = refs[2 * pieces :]
    rows, width = h_ref.shape
    local = do_ref.shape[1]
    for k, group in enumerate((mine, theirs)):
        for copy in row_copies(group, c_ref[1], width, w_scr.at[k], slice(0, 256), sem.at[k]):
            copy.start()
    n2, r2 = normalize(h_ref[...])
    dc = own_ref[...].astype(f32) + recv_ref[...].astype(f32)
    token = ((2 * part) ^ c_ref[0]) * rows + lax.broadcasted_iota(jnp.int32, (rows, 1), 0)
    g = jnp.where(token < c_ref[3], g_ref[...].astype(f32), 0.0)
    dh = g + norm_back(dc, n2, r2, norm_ref[1:2, :])
    dh_ref[...] = dh
    dhb = dh.astype(bf)
    dhb_ref[...] = dhb
    sum_ref[0:1, :] = jnp.sum(dc * n2, axis=0, keepdims=True)
    sum_ref[1:2, :] = jnp.sum(dc, axis=0, keepdims=True)
    sum_ref[2:8, :] = jnp.zeros((6, width), f32)
    for k in range(2):
        wait_for(w_scr.at[k], sem.at[k])
        do_ref[k] = dot(dhb, w_scr[k]).T[0:local].astype(bf)


def middle(part, scalars, h, own, recv, g, norms, mine, theirs, local):
    rows, width = h.shape
    spec = pltpu.PrefetchScalarGridSpec(
        num_scalar_prefetch=1,
        grid=(1,),
        in_specs=[whole(h.shape)] * 3 + [pl.BlockSpec((rows, width), lambda i, c: ((2 * part) ^ c[0], 0)), whole(norms.shape)] + [ANY] * (2 * len(mine)),
        out_specs=[whole(h.shape), whole(h.shape), whole((2, local, rows)), whole((8, width))],
        scratch_shapes=[pltpu.VMEM((2, width, 256), bf), pltpu.SemaphoreType.DMA((2,))],
    )
    return pl.pallas_call(
        functools.partial(middle_kernel, part, len(mine)),
        grid_spec=spec,
        out_shape=[SDS(h.shape, f32), SDS(h.shape, bf), SDS((2, local, rows), bf), SDS((8, width), f32)],
        compiler_params=params(),
        cost_estimate=cost(4 * rows * width * 256, 8 << 20),
        name=f"middle{part}",
    )(scalars, h, own, recv, g, norms, *mine, *theirs)


def relative_rows(scr, d, index, count, relative):
    r = count // 8
    y, s = index // 4, index % 4
    at = pl.multiple_of((d ^ (2 * s + y)) * r, r) if relative else index * r
    return scr[pl.ds(at, r), :]


def weight_grad_kernel(first, relative, k, c_ref, *refs):
    if first:
        src, (e1, e2, du1, du2, o1, o2, grad_ref, turned_ref, scr, w_scr) = refs[:6], refs[6:]
        rows, width = src[0].shape
        for j in range(3):
            for i in range(2):
                scr[:, i * rows : (i + 1) * rows] = src[2 * j + i][...].T
            for b in range(8):
                r = width // 8
                turned_ref[j, b * r : (b + 1) * r, :] = relative_rows(scr, c_ref[1], b, width, relative)
    else:
        turned_ref, e1, e2, du1, du2, o1, o2, recv_ref, grad_ref = refs
        width = turned_ref.shape[1]
        rows = turned_ref.shape[2] // 2
    units = du1.shape[2]
    local = o1.shape[-2]
    a, b = slice(0, rows), slice(rows, 2 * rows)
    o_at = (0,) if len(o1.shape) == 3 else ()
    up = dot(turned_ref[0, :, a], du1[k]) + dot(turned_ref[0, :, b], du2[k])
    down = dot(turned_ref[1, :, a], e1[k]) + dot(turned_ref[1, :, b], e2[k])
    out = dot(turned_ref[2, :, a], o1[o_at + (Ellipsis,)], NT) + dot(turned_ref[2, :, b], o2[o_at + (Ellipsis,)], NT)
    out = jnp.concatenate([out, jnp.zeros((width, 256 - local), f32)], axis=1)
    for at, value in ((slice(0, units), up), (slice(units, 2 * units), down), (slice(2 * units, 2 * units + 256), out)):
        if not first:
            value = value + recv_ref[:, at].astype(f32)
        grad_ref[:, at] = value.astype(bf)


def weight_grad_first(scalars, relative, cs, gbs, dhbs, es, dus, others):
    rows, width = cs[0].shape
    units = es[0].shape[2]
    ins = [*cs, *gbs, *dhbs, *es, *dus, *others]
    spec = pltpu.PrefetchScalarGridSpec(
        num_scalar_prefetch=1,
        grid=(1,),
        in_specs=[whole(v.shape) for v in ins],
        out_specs=[whole((width, 2 * units + 256)), whole((3, width, 2 * rows))],
        scratch_shapes=[pltpu.VMEM((width, 2 * rows), bf), pltpu.VMEM((8, 128), f32)],
    )
    return pl.pallas_call(
        functools.partial(weight_grad_kernel, True, relative, 1),
        grid_spec=spec,
        out_shape=[SDS((width, 2 * units + 256), bf), SDS((3, width, 2 * rows), bf)],
        compiler_params=params(),
        cost_estimate=cost(10 * rows * width * units, 18 << 20),
        name="weight_grad_first",
    )(scalars, *ins)


def weight_grad_second(scalars, turned, es, dus, os, recv):
    _, width, tokens = turned.shape
    units = es[0].shape[2]
    ins = [turned, *es, *dus, *os, recv]
    spec = pltpu.PrefetchScalarGridSpec(
        num_scalar_prefetch=1,
        grid=(1,),
        in_specs=[whole(v.shape) for v in ins],
        out_specs=whole((width, 2 * units + 256)),
    )
    return pl.pallas_call(
        functools.partial(weight_grad_kernel, False, False, 0),
        grid_spec=spec,
        out_shape=SDS((width, 2 * units + 256), bf),
        compiler_params=params(),
        cost_estimate=cost(5 * tokens * width * units, 18 << 20),
        name="weight_grad_second",
    )(scalars, *ins)


def attend_back_kernel(part, chunk, c_ref, kp_ref, vp_ref, kt_ref, qt_ref, o_ref, lse_ref, do_ref, *refs):
    if part == 0:
        dq_ref, dk_ref, dv_ref = refs
    else:
        dk_in, dv_in, dq_ref, out_ref, dk_ref, dv_ref = refs
    q = qt_ref.shape[1]
    keys = kp_ref.shape[0]
    step = pl.program_id(1)

    @pl.when(step == 0)
    def _():
        if part == 0:
            dk_ref[...] = jnp.zeros_like(dk_ref)
            dv_ref[...] = jnp.zeros_like(dv_ref)
        else:
            dk_ref[...] = dk_in[...]
            dv_ref[...] = dv_in[...]

    qt = qt_ref[...]
    do = do_ref[0]
    delta = jnp.sum(do.astype(f32) * o_ref[0].astype(f32), axis=0, keepdims=True)
    one = jnp.ones((1, q), f32)
    queries = with_tail(qt, [one] + [-v for v in split3(lse_ref[0, 0, 0:1])])
    grads = with_tail(do, [0.0 * one] + [-v for v in split3(delta)])
    dq = None
    for i in range(keys // chunk):
        at = slice(i * chunk, (i + 1) * chunk)
        p = jnp.exp2(dot(kp_ref[at, :], queries) * LOG2E)
        dp = dot(vp_ref[at, :], grads)
        ds = (p * dp).astype(bf)
        dv_ref[0, at, :] += dot(p.astype(bf), do, NT)
        dk_ref[0, at, :] += dot(ds, qt, NT)
        here = dot(kt_ref[:, at], ds)
        dq = here if dq is None else dq + here
    dq_ref[0] = (dq * 0.125).astype(bf)
    if part == 1:

        @pl.when(step == 1)
        def _():
            for m in range(4):
                at = pl.ds(pl.multiple_of((m ^ c_ref[0]) * q, q), q)
                out_ref[m % 2, m // 2, 0] = dk_ref[0, at, :].T.astype(bf)
                out_ref[m % 2, m // 2, 1] = dv_ref[0, at, :].T.astype(bf)


def attend_back(part, scalars, kp, vp, kt, qt, o, lse, do, sums=()):
    count = kp.shape[0]
    heads = qt.shape[0] // HD
    q = count // 4
    keyed = pl.BlockSpec((count, 2 * HD), lambda h, i, c: (0, h))
    block = pl.BlockSpec((1, HD, q), lambda h, i, c: (i, h, 0))
    total = pl.BlockSpec((1, count, HD), lambda h, i, c: (h, 0, 0))
    total_shape = SDS((heads, count, HD), f32)
    dq_shape = SDS((2, heads * HD, q), bf)
    if part == 0:
        out_specs, out_shape, scratch = [block, total, total], [dq_shape, total_shape, total_shape], []
    else:
        out_specs = [block, pl.BlockSpec((2, 2, 2, HD, q), lambda h, i, c: (0, 0, 0, h, 0))]
        out_shape = [dq_shape, SDS((2, 2, 2, heads * HD, q), bf)]
        scratch = [pltpu.VMEM((1, count, HD), f32)] * 2
    spec = pltpu.PrefetchScalarGridSpec(
        num_scalar_prefetch=1,
        grid=(heads, 2),
        in_specs=[
            keyed,
            keyed,
            pl.BlockSpec((HD, count), lambda h, i, c: (h, 0)),
            pl.BlockSpec((HD, q), lambda h, i, c: (h, (2 * part + i) ^ c[0])),
            block,
            pl.BlockSpec((1, 1, 8, q), lambda h, i, c: (h, i, 0, 0)),
            block,
        ]
        + [total] * len(sums),
        out_specs=out_specs,
        scratch_shapes=scratch,
    )
    return pl.pallas_call(
        functools.partial(attend_back_kernel, part, min(512, count)),
        grid_spec=spec,
        out_shape=out_shape,
        compiler_params=params(),
        cost_estimate=cost(heads * 5 * count * count * 256, heads * count * 2048, heads * count * count // 2),
        name=f"attend_back{part}",
    )(scalars, kp, vp, kt, qt, o, lse, do, *sums)


def da_kernel(pieces, c_ref, dq1, dq2, dkv, rq1, rq2, rkv, *refs):
    mine, theirs = refs[:pieces], refs[pieces : 2 * pieces]
    one_ref, two_ref, w_scr, d_scr, sem = refs[2 * pieces :]
    width = one_ref.shape[0]
    local = rq1.shape[0]
    for k, group in enumerate((mine, theirs)):
        for copy in row_copies(group, c_ref[1], width, w_scr.at[k], slice(0, 3 * local), sem.at[k]):
            copy.start()
    for i, out_ref in enumerate((one_ref, two_ref)):
        own, other = (dq1, dq2)[i], (rq1, rq2)[i]
        d_scr[i, 0, 0:local, :] = own[0]
        d_scr[i, 1, 0:local, :] = other[...]
        for j in range(2):
            at = slice((j + 1) * local, (j + 2) * local)
            d_scr[i, 0, at, :] = dkv[0, i, j]
            d_scr[i, 1, at, :] = rkv[i, j]
    for k in range(2):
        wait_for(w_scr.at[k], sem.at[k])
    for i, out_ref in enumerate((one_ref, two_ref)):
        out_ref[...] = (dot(w_scr[0], d_scr[i, 0]) + dot(w_scr[1], d_scr[i, 1])).astype(bf)


def da_product(scalars, dq1, dq2, dkv, rq1, rq2, rkv, mine, theirs, width):
    local, q = rq1.shape
    ins = [dq1, dq2, dkv, rq1, rq2, rkv]
    spec = pltpu.PrefetchScalarGridSpec(
        num_scalar_prefetch=1,
        grid=(1,),
        in_specs=[whole(v.shape) for v in ins] + [ANY] * (2 * len(mine)),
        out_specs=[whole((width, q))] * 2,
        scratch_shapes=[pltpu.VMEM((2, width, 3 * local), bf), pltpu.VMEM((2, 2, 3 * local, q), bf), pltpu.SemaphoreType.DMA((2,))],
    )
    return pl.pallas_call(
        functools.partial(da_kernel, len(mine)),
        grid_spec=spec,
        out_shape=[SDS((width, q), bf)] * 2,
        compiler_params=params(),
        cost_estimate=cost(24 * local * width * q, 8 << 20),
        name="da_product",
    )(scalars, *ins, *mine, *theirs)


def dx_kernel(c_ref, own_ref, recv_ref, x_ref, dh_ref, norm_ref, dx_ref, sum_ref):
    width = norm_ref.shape[1]
    da = (own_ref[...].astype(f32) + recv_ref[...].astype(f32)).T
    n1, r1 = normalize(x_ref[...].astype(f32))
    dx_ref[...] = (dh_ref[...] + norm_back(da, n1, r1, norm_ref[0:1, :])).astype(bf)
    sum_ref[0:1, :] = jnp.sum(da * n1, axis=0, keepdims=True)
    sum_ref[1:2, :] = jnp.sum(da, axis=0, keepdims=True)
    sum_ref[2:8, :] = jnp.zeros((6, width), f32)


def dx_block(part, scalars, own, recv, x, dh, norms):
    width, rows = own.shape
    spec = pltpu.PrefetchScalarGridSpec(
        num_scalar_prefetch=1,
        grid=(1,),
        in_specs=[whole(own.shape)] * 2
        + [pl.BlockSpec((rows, width), lambda i, c: ((2 * part) ^ c[0], 0)), whole(dh.shape), whole(norms.shape)],
        out_specs=[whole((rows, width)), whole((8, width))],
    )
    return pl.pallas_call(
        dx_kernel,
        grid_spec=spec,
        out_shape=[SDS((rows, width), bf), SDS((8, width), f32)],
        compiler_params=params(),
        cost_estimate=cost(20 * rows * width, 6 << 20),
        name=f"dx{part}",
    )(scalars, own, recv, x, dh, norms)


def qkv_grad_kernel(relative, c_ref, a_ref, dq1, dq2, dkv, grad_ref, g_scr):
    local, q = dq1.shape[1:]
    width = a_ref.shape[1]
    total = [None] * 3
    for m in range(4):
        a = a_ref[m * q : (m + 1) * q, :]
        parts = [(dq1, dq2)[m // 2][m % 2], dkv[m % 2, m // 2, 0], dkv[m % 2, m // 2, 1]]
        for j in range(3):
            here = dot(parts[j], a)
            total[j] = here if total[j] is None else total[j] + here
    for j in range(3):
        g_scr[:, j * local : (j + 1) * local] = total[j].T.astype(bf)
    r = width // 8
    for b in range(8):
        grad_ref[b * r : (b + 1) * r, :] = relative_rows(g_scr, c_ref[1], b, width, relative)


def qkv_grad(scalars, relative, normed, dq1, dq2, dkv):
    width = normed.shape[1]
    local = dq1.shape[1]
    ins = [normed, dq1, dq2, dkv]
    spec = pltpu.PrefetchScalarGridSpec(
        num_scalar_prefetch=1,
        grid=(1,),
        in_specs=[whole(v.shape) for v in ins],
        out_specs=whole((width, 3 * local)),
        scratch_shapes=[pltpu.VMEM((width, 3 * local), bf)],
    )
    return pl.pallas_call(
        functools.partial(qkv_grad_kernel, relative),
        grid_spec=spec,
        out_shape=SDS((width, 3 * local), bf),
        compiler_params=params(),
        cost_estimate=cost(6 * normed.shape[0] * width * local, 8 << 20),
        name="qkv_grad",
    )(scalars, *ins)


def gather_z(piece, n):
    return jnp.stack([piece] + [swap(piece, "dp", 2 * s, n) for s in (1, 2, 3)])


def scatter_rows(value, n):
    if n != 8:
        return lax.psum_scatter(value, "dp", scatter_dimension=0, tiled=True).astype(f32)
    r = value.shape[0] // 8
    keep, send = value[: 4 * r], value[4 * r :]
    half = (keep.astype(f32) + swap(send, "dp", 1, n).astype(f32)).astype(bf)
    total = half[0:r].astype(f32)
    for s in (1, 2, 3):
        total = total + swap(half[s * r : (s + 1) * r], "dp", 2 * s, n).astype(f32)
    return total


def sum_everywhere(value, n):
    value = value + core_swap(value)
    if n != 8:
        return lax.psum(value, "dp")
    value = value + swap(value, "dp", 1, n)
    return value + swap(value, "dp", 2, n) + swap(value, "dp", 4, n) + swap(value, "dp", 6, n)


def in_order(c, first, first_other, second, second_other):
    one = jnp.where(c == 0, jnp.concatenate([first, first_other]), jnp.concatenate([first_other, first]))
    two = jnp.where(c == 0, jnp.concatenate([second, second_other]), jnp.concatenate([second_other, second]))
    return jnp.concatenate([one, two])


def body(n, embeddings, cotangent, species, gene_ids, w_qkv, w_out, w_up, w_down, norm_gains, norm_shifts):
    c = lax.axis_index("tensor") % 2
    d = lax.axis_index("dp")
    relative = n == 8
    count, width = embeddings.shape
    r = width // n
    local = w_qkv.shape[2]
    units = w_up.shape[1]
    length = jnp.sum((gene_ids != 0).astype(jnp.int32))
    alive = jnp.where(species[0] == 2, 0, length)
    scalars = jnp.stack([c, d, length, alive]).astype(jnp.int32)

    qkv_own = jnp.concatenate([w_qkv[j].astype(bf) for j in range(3)], axis=1)
    norms_own = jnp.concatenate([norm_gains, norm_shifts]).astype(bf)
    out_own = jnp.pad(w_out.astype(bf).T, ((0, 0), (0, 256 - local)))
    up_own = w_up.astype(bf)
    down_own = w_down.astype(bf).T
    if relative:
        spread = lax.dynamic_update_slice(jnp.zeros((4, width), bf), norms_own, (0, d * r))
        spread = spread.reshape(4, 2, width // 2).transpose(1, 0, 2).reshape(8, width // 2)
        spread = jnp.pad(spread, ((0, 8), (0, 3 * local - width // 2)))
        first_z = gather_z(jnp.concatenate([qkv_own, spread]), n)
        w_first = [first_z, swap(first_z, "dp", 1, n)]
        norms = None
        out_own = after(out_own, first_z)
        out_z = gather_z(out_own, n)
        w_o = [out_z, swap(out_z, "dp", 1, n)]
        up_z = gather_z(after(up_own, first_z), n)
        w_u = [up_z, swap(up_z, "dp", 1, n)]
        down_z = gather_z(after(down_own, out_z), n)
        w_d = [down_z, swap(down_z, "dp", 1, n)]
    else:
        rows = lambda v: [lax.all_gather(v, "dp", axis=0, tiled=True)]
        w_first, w_o, w_u, w_d = rows(qkv_own), rows(out_own), rows(up_own), rows(down_own)
        norms = lax.all_gather(norms_own, "dp", axis=1, tiled=True)
        norms = norms.reshape(4, 2, width // 2).transpose(1, 0, 2).reshape(8, width // 2)
        norms = jnp.pad(norms, ((0, 8), (0, 3 * local - width // 2)))
    others = lambda group: [core_swap(v) for v in group]

    normed, kp, vp, kt, vt, qt, norm_rows = project(scalars, embeddings, w_first, norms, local)
    w_o2, w_u2, w_d2 = others(w_o), others(w_u), others(w_d)
    o, lse, o_other, h, cs, gbs, es, dus, ffns, dcs = ([None] * 2 for _ in range(10))
    sent = [None] * 2
    for i in range(2):
        o[i], lse[i] = attend(scalars, kp, vt, qt, i)
        o_other[i] = core_swap(o[i][1])
        sent[i] = out_product(scalars, o[i], o_other[i], w_o, w_o2, width)
    for i in range(2):
        recv = x_swap(sent[i])
        h[i], cs[i], gbs[i], es[i], dus[i], ffns[i], dcs[i] = ffn(
            i, scalars, embeddings, cotangent, sent[i], recv, norm_rows, w_u, w_d, w_u2, w_d2, units
        )
    dh, dhb, do, sums = ([None] * 2 for _ in range(4))
    for i in range(2):
        recv = x_swap(dcs[i])
        dh[i], dhb[i], do[i], sums[i] = middle(i, scalars, h[i], dcs[i], recv, cotangent, norm_rows, w_o, w_o2, local)
        do[i] = jnp.stack([do[i][0], core_swap(do[i][1])])
    dq1, dk, dv = attend_back(0, scalars, kp, vp, kt, qt, o[0], lse[0], do[0])
    grad_theirs, turned = weight_grad_first(scalars, relative, cs, gbs, dhb, es, dus, o_other)
    grad_ours = weight_grad_second(scalars, turned, es, dus, o, core_swap(grad_theirs))
    s_rest = scatter_rows(grad_ours, n)
    dq2, dkv = attend_back(1, scalars, kp, vp, kt, qt, o[1], lse[1], do[1], (dk, dv))

    ffns = [after(v, dcs[1]) for v in ffns]
    mixed = [(h[i] + (ffns[i].astype(f32) + x_swap(ffns[i]).astype(f32))).astype(bf) for i in range(2)]
    mixed = in_order(c, mixed[0], core_swap(mixed[0]), mixed[1], core_swap(mixed[1]))

    rq1, rq2, rkv = core_swap(dq1[1]), core_swap(dq2[1]), core_swap(dkv[1])
    w_first2 = others(w_first)
    da = da_product(scalars, dq1, dq2, dkv, rq1, rq2, rkv, w_first, w_first2, width)
    grad_first = qkv_grad(scalars, relative, normed, dq1, dq2, dkv)
    s_first = scatter_rows(grad_first, n)
    dx, sums1 = [None] * 2, [None] * 2
    for i in range(2):
        dx[i], sums1[i] = dx_block(i, scalars, da[i], x_swap(da[i]), embeddings, dh[i], norm_rows)
    grad_input = in_order(c, dx[0], core_swap(dx[0]), dx[1], core_swap(dx[1]))
    both = jnp.concatenate([(sums1[0] + sums1[1])[0:2], (sums[0] + sums[1])[0:2]])
    both = lax.dynamic_slice(sum_everywhere(both, n), (0, d * r), (4, r))
    s_qkv = s_first.reshape(r, 3, local).transpose(1, 0, 2)
    s_up, s_down, s_out = s_rest[:, :units], s_rest[:, units : 2 * units].T, s_rest[:, 2 * units : 2 * units + local].T
    gains = jnp.stack([both[0], both[2]])
    shifts = jnp.stack([both[1], both[3]])
    return (mixed, grad_input, s_qkv, s_out, s_up, s_down, gains, shifts, both[3])


def solution(mesh):
    return jax.shard_map(
        functools.partial(body, mesh.shape["dp"]),
        mesh=mesh,
        in_specs=(
            P("dp", None),
            P("dp", None),
            P("dp"),
            P("dp", None),
            P(None, "dp", "tensor"),
            P("tensor", "dp"),
            P("dp", "tensor"),
            P("tensor", "dp"),
            P(None, "dp"),
            P(None, "dp"),
        ),
        out_specs=(
            P("dp", None),
            P("dp", None),
            P(None, "dp", "tensor"),
            P("tensor", "dp"),
            P("dp", "tensor"),
            P("tensor", "dp"),
            P(None, "dp"),
            P(None, "dp"),
            P("dp"),
        ),
        check_vma=False,
    )
```

time: 989 us -> 409 us (0.41)
  waiting for transfers between devices: 532 us -> 140 us
  matrix products: 187 us -> 0 us
  Pallas kernels: 0 us -> 164 us
  blocking collectives: 107 us -> 0 us
  other arithmetic: 84.5 us -> 18.5 us
  starting transfers between devices: 1.09 us -> 56 us
  local copies, waits for them, and re-layouts: 54.7 us -> 20 us
  between operations: 16.9 us -> 3.19 us
    psum x3 -> x0, waiting for transfers between devices: 240 us -> none  [the longest x1 115 us: body(): lax.psum(ffn_part, 'tensor').astype(jnp.float32)]
    dot_general x38 -> x0, matrix products: 179 us -> none  [the longest x4 22.6 us: visit(): jnp.einsum('hqk,khe->qhe', grad_scores, key_rows, preferred_element_type=...]
    pallas_call x0 -> x17, Pallas kernels: none -> 164 us  [the longest x2 38.9 us: attend_back(): pl.pallas_call(functools.partial(attend_back_kernel, part, min(512, count...]
    unnamed x15 -> x0, waiting for transfers between devices: 150 us -> none
    reduce_scatter x2 -> x0, waiting for transfers between devices: 142 us -> none  [the longest x1 72.1 us: body(): lax.psum_scatter(grad_down, 'dp', scatter_dimension=1, tiled=True)]
    ppermute x0 -> x57, waiting for transfers between devices: none -> 140 us  [swap(): return lax.ppermute(value, axis, [(i, i ^ mask) for i in range(size)])]
    all_gather x4 -> x0, blocking collectives: 107 us -> none  [the longest x1 36.7 us: body(): lax.all_gather(w_qkv.astype(bfloat), 'dp', axis=1, tiled=True)]
    ppermute x0 -> x57, starting transfers between devices: none -> 56 us  [swap(): return lax.ppermute(value, axis, [(i, i ^ mask) for i in range(size)])]
  transfers between devices with their start and end apart: 11 -> 57, of which waited for: 8 -> 21; matrix products, arithmetic and copies ran while one was open for 10% -> 5% of each run, Pallas kernels for 0% -> 41%
where the time goes in v2:
time: 409 us; the launch traced here: 401 us
  Pallas kernels  164 us (40%)
  waiting for transfers between devices  140 us (34%)
  starting transfers between devices  56 us (14%)
  local copies, waits for them, and re-layouts  20 us (5%)
  other arithmetic  18.5 us (5%)
    ppermute x57, waiting for transfers between devices, swap(): return lax.ppermute(value, axis, [(i, i ^ mask) for i in range(size)])  140 us
    ppermute x57, starting transfers between devices, swap(): return lax.ppermute(value, axis, [(i, i ^ mask) for i in range(size)])  56 us
    pallas_call x2, Pallas kernels, attend_back(): pl.pallas_call(functools.partial(attend_back_kernel, part, min(512, count...  38.9 us
    pallas_call x2, Pallas kernels, ffn(): pl.pallas_call(functools.partial(ffn_kernel, part, len(up)), grid_spec=sp...  35.3 us
    pallas_call x2, Pallas kernels, attend(): pl.pallas_call(functools.partial(attend_kernel, min(512, count)), grid_sp...  23.3 us
    unnamed x95, local copies, waits for them, and re-layouts  15.6 us
    pallas_call x2, Pallas kernels, middle(): pl.pallas_call(functools.partial(middle_kernel, part, len(mine)), grid_sp...  12.3 us
    pallas_call x1, Pallas kernels, project(): pl.pallas_call(functools.partial(project_kernel, heads, len(w)), grid_spe...  11.6 us
  transfers between devices with their start and end apart: 57, of which 21 were waited for; matrix products, arithmetic and copies ran while one was open for 5% of the time, Pallas kernels for 41%

profile of v2, /device:TPU:0, one launch (start us, length us, event | category | flops | bytes accessed | tf_op | source)
XLA Modules:
  0.0 401.5 jit_solution(3078220901472572462)
XLA Ops:
  10.3 5.6 %collective-permute-done.1 = bf16[112,576]{1,0:T(8,128)(2,1)S(1)} collective-permute-done((bf16[112,576]{1,0:T(8,128)(2,1)S(1)}, bf16[112,576]{1,0:T(8,128)(2,1)S(1)}, u32[]{:S(2)}, u32[]{:S(2)}) %collective-permute-start.1) | collective-permute-done | bytes 129056 | tf_op jit(solution)/shard_map/ppermute | solution.py:28
  41.1 6.5 %collective-permute-done.13 = bf16[96,768]{1,0:T(8,128)(2,1)S(1)} collective-permute-done((bf16[96,768]{1,0:T(8,128)(2,1)S(1)}, bf16[96,768]{1,0:T(8,128)(2,1)S(1)}, u32[]{:S(2)}, u32[]{:S(2)}) %collective-permute-start.13) | collective-permute-done | bytes 147488 | tf_op jit(solution)/shard_map/ppermute | solution.py:28
  57.4 11.6 %project.1 = (bf16[2048,768]{1,0:T(8,128)(2,1)}, bf16[2048,384]{1,0:T(8,128)(2,1)S(1)}, bf16[2048,384]{1,0:T(8,128)(2,1)}, bf16[192,2048]{1,0:T(8,128)(2,1)S(1)}...) custom-call(s32[4]{0:T(128)S(1)} %pad_add_fusion.c_ref, ...), custom_call_target="tpu_custom_call" | custom-call | flops 4227858432 | bytes 25165824 | tf_op jit(solution)/shard_map/project/pallas_call | solution.py:176
  69.0 11.7 %attend1.1 = (bf16[2,192,512]{2,1,0:T(8,128)(2,1)S(1)}, f32[3,2,8,512]{3,2,1,0:T(8,128)S(1)}) custom-call(s32[4]{0:T(128)S(1)} %pad_add_fusion.c_ref, bf16[2048,384]{1,0:T(8,128)(2,1)S(1)} %get-tuple-element.60.kp_ref, bf16[192,2048]{1,0:T(8,128)(2,1)S(1)} %get-tuple-element.61.vt_ref, bf16[192,2048]{1,0:T(8,128)(2,1)S(1)} %get-tuple-element.62.qt_ref), custom_call_target="tpu_custom_call" | custom-call | flops 6442450944 | bytes 3145728 | tf_op jit(solution)/shard_map/attend1/pallas_call | solution.py:230
  80.8 11.7 %attend0.1 = (bf16[2,192,512]{2,1,0:T(8,128)(2,1)S(1)}, f32[3,2,8,512]{3,2,1,0:T(8,128)S(1)}) custom-call(s32[4]{0:T(128)S(1)} %pad_add_fusion.c_ref, bf16[2048,384]{1,0:T(8,128)(2,1)S(1)} %get-tuple-element.60.kp_ref, bf16[192,2048]{1,0:T(8,128)(2,1)S(1)} %get-tuple-element.61.vt_ref, bf16[192,2048]{1,0:T(8,128)(2,1)S(1)} %get-tuple-element.62.qt_ref), custom_call_target="tpu_custom_call" | custom-call | flops 6442450944 | bytes 3145728 | tf_op jit(solution)/shard_map/attend0/pallas_call | solution.py:230
  101.6 15.2 %collective-permute-done.25.recv_ref = bf16[768,512]{1,0:T(8,128)(2,1)S(1)} collective-permute-done((bf16[768,512]{1,0:T(8,128)(2,1)S(1)}, bf16[768,512]{1,0:T(8,128)(2,1)S(1)}, u32[]{:S(2)}, u32[]{:S(2)}) %collective-permute-start.25) | collective-permute-done | bytes 786464 | tf_op jit(solution)/shard_map/ppermute | solution.py:28
  117.7 17.5 %ffn1.1 = (f32[512,768]{1,0:T(8,128)}, bf16[512,768]{1,0:T(8,128)(2,1)S(1)}, bf16[512,768]{1,0:T(8,128)(2,1)}, bf16[2,512,768]{2,1,0:T(8,128)(2,1)}, bf16[2,512,...) custom-call(s32[4]{0:T(128)S(1)} %pad_add_fusion.c_ref, bf16[2048,768]{1,0:T(8,128)(2,1)} %x_ref.9, ...), custom_call_target="tpu_custom_call" | custom-call | flops 4831838208 | bytes 16777216 | tf_op jit(solution)/shard_map/ffn1/pallas_call | solution.py:317
  138.5 17.7 %ffn0.1 = (f32[512,768]{1,0:T(8,128)}, bf16[512,768]{1,0:T(8,128)(2,1)S(1)}, bf16[512,768]{1,0:T(8,128)(2,1)}, bf16[2,512,768]{2,1,0:T(8,128)(2,1)}, bf16[2,512,...) custom-call(s32[4]{0:T(128)S(1)} %pad_add_fusion.c_ref, bf16[2048,768]{1,0:T(8,128)(2,1)} %x_ref.9, ...), custom_call_target="tpu_custom_call" | custom-call | flops 4831838208 | bytes 16777216 | tf_op jit(solution)/shard_map/ffn0/pallas_call | solution.py:317
  163.7 5.8 %middle1.1 = (f32[512,768]{1,0:T(8,128)S(1)}, bf16[512,768]{1,0:T(8,128)(2,1)S(1)}, bf16[2,192,512]{2,1,0:T(8,128)(2,1)S(1)}, f32[8,768]{1,0:T(8,128)S(1)}) custom-call(s32[4]{0:T(128)S(1)} %pad_add_fusion.c_ref, f32[512,768]{1,0:T(8,128)} %get-tuple-element.73.h_ref, bf16[512,768]{1,0:T(8,128)(2,1)S(1)} %copy-done.14, bf16[512,768]{1,0:T(8,128)(2,1)S(1)} %copy-done.16, ...), custom_call_target="tpu_custom_call" | custom-call | flops 402653184 | bytes 8388608 | tf_op jit(solution)/shard_map/middle1/pallas_call | solution.py:362
  169.6 8.4 %collective-permute-done.30.recv_ref = bf16[512,768]{1,0:T(8,128)(2,1)} collective-permute-done((bf16[512,768]{1,0:T(8,128)(2,1)}, bf16[512,768]{1,0:T(8,128)(2,1)}, u32[]{:S(2)}, u32[]{:S(2)}) %collective-permute-start.30) | collective-permute-done | bytes 786464 | tf_op jit(solution)/shard_map/ppermute | solution.py:28
  178.0 6.5 %middle0.1 = (f32[512,768]{1,0:T(8,128)S(1)}, bf16[512,768]{1,0:T(8,128)(2,1)S(1)}, bf16[2,192,512]{2,1,0:T(8,128)(2,1)S(1)}, f32[8,768]{1,0:T(8,128)S(1)}) custom-call(s32[4]{0:T(128)S(1)} %pad_add_fusion.c_ref, f32[512,768]{1,0:T(8,128)} %get-tuple-element.68.h_ref, bf16[512,768]{1,0:T(8,128)(2,1)S(1)} %copy-done.13, ...), custom_call_target="tpu_custom_call" | custom-call | flops 402653184 | bytes 8388608 | tf_op jit(solution)/shard_map/middle0/pallas_call | solution.py:362
  185.9 10.2 %weight_grad_first.1 = (bf16[768,1792]{1,0:T(8,128)(2,1)}, bf16[3,768,1024]{2,1,0:T(8,128)(2,1)}) custom-call(s32[4]{0:T(128)S(1)} %pad_add_fusion.c_ref, bf16[512,768]{1,0:T(8,128)(2,1)S(1)} %copy-done.9, bf16[512,768]{1,0:T(8,128)(2,1)S(1)} %copy-done.6, bf16[512,768]{1,0:T(8,128)(2,1)S(1)} %copy-done.10, bf16[512,768]{1,0:T(8,128)(2,1)S(1)} %copy-done.7, ...), custom_call_target="tpu_custom_call" | custom-call | flops 3019898880 | bytes 18874368 | tf_op jit(solution)/shard_map/weight_grad_first/pallas_call | solution.py:418
  199.5 18.8 %attend_back0.1 = (bf16[2,192,512]{2,1,0:T(8,128)(2,1)S(1)}, f32[3,2048,64]{2,1,0:T(8,128)}, f32[3,2048,64]{2,1,0:T(8,128)}) custom-call(s32[4]{0:T(128)S(1)} %pad_add_fusion.c_ref, bf16[2048,384]{1,0:T(8,128)(2,1)S(1)} %copy-done.26, bf16[2048,384]{1,0:T(8,128)(2,1)S(1)} %copy-done.27, bf16[192,2048]{1,0:T(8,128)(2,1)S(1)} %copy-done.29, ...), custom_call_target="tpu_custom_call" | custom-call | flops 16106127360 | bytes 12582912 | tf_op jit(solution)/shard_map/attend_back0/pallas_call | solution.py:524
  218.3 20.1 %attend_back1.1 = (bf16[2,192,512]{2,1,0:T(8,128)(2,1)S(1)}, bf16[2,2,2,192,512]{4,3,2,1,0:T(8,128)(2,1)S(1)}) custom-call(s32[4]{0:T(128)S(1)} %pad_add_fusion.c_ref, bf16[2048,384]{1,0:T(8,128)(2,1)S(1)} %copy-done.26, bf16[2048,384]{1,0:T(8,128)(2,1)} %get-tuple-element.76.vp_ref, bf16[192,2048]{1,0:T(8,128)(2,1)S(1)} %copy-done.29, ...), custom_call_target="tpu_custom_call" | custom-call | flops 16106127360 | bytes 12582912 | tf_op jit(solution)/shard_map/attend_back1/pallas_call | solution.py:524
  238.4 4.8 %qkv_grad.1 = bf16[768,576]{1,0:T(8,128)(2,1)S(1)} custom-call(s32[4]{0:T(128)S(1)} %pad_add_fusion.c_ref, bf16[2048,768]{1,0:T(8,128)(2,1)} %get-tuple-element.94.a_ref, bf16[2,192,512]{2,1,0:T(8,128)(2,1)S(1)} %get-tuple-element.81.dq1, bf16[2,192,512]{2,1,0:T(8,128)(2,1)S(1)} %get-tuple-element.86.dq2, bf16[2,2,2,192,512]{4,3,2,1,0:T(8,128)(2,1)S(1)} %get-tuple-element.87.dkv), custom_call_target="tpu_custom_call" | custom-call | flops 1811939328 | bytes 8388608 | tf_op jit(solution)/shard_map/qkv_grad/pallas_call | solution.py:633
  245.1 11.4 %collective-permute-done.43 = bf16[384,576]{1,0:T(8,128)(2,1)S(1)} collective-permute-done((bf16[384,576]{1,0:T(8,128)(2,1)S(1)}, bf16[384,576]{1,0:T(8,128)(2,1)S(1)}, u32[]{:S(2)}, u32[]{:S(2)}) %collective-permute-start.43) | collective-permute-done | bytes 442400 | tf_op jit(solution)/shard_map/ppermute | solution.py:28
  259.0 7.5 %da_product.1 = (bf16[768,512]{1,0:T(8,128)(2,1)}, bf16[768,512]{1,0:T(8,128)(2,1)S(1)}) custom-call(s32[4]{0:T(128)S(1)} %pad_add_fusion.c_ref, bf16[2,192,512]{2,1,0:T(8,128)(2,1)S(1)} %get-tuple-element.81.dq1, bf16[2,192,512]{2,1,0:T(8,128)(2,1)S(1)} %get-tuple-element.86.dq2, bf16[2,2,2,192,512]{4,3,2,1,0:T(8,128)(2,1)} %copy-done.19, ...), custom_call_target="tpu_custom_call" | custom-call | flops 1811939328 | bytes 8388608 | tf_op jit(solution)/shard_map/da_product/pallas_call | solution.py:566
  268.6 8.4 %collective-permute-done.26 = bf16[512,768]{1,0:T(8,128)(2,1)S(1)} collective-permute-done((bf16[512,768]{1,0:T(8,128)(2,1)S(1)}, bf16[512,768]{1,0:T(8,128)(2,1)S(1)}, u32[]{:S(2)}, u32[]{:S(2)}) %collective-permute-start.26) | collective-permute-done | bytes 786464 | tf_op jit(solution)/shard_map/ppermute | solution.py:28
  299.0 9.9 %collective-permute-done.41.recv_ref = bf16[768,512]{1,0:T(8,128)(2,1)} collective-permute-done((bf16[768,512]{1,0:T(8,128)(2,1)S(1)}, bf16[768,512]{1,0:T(8,128)(2,1)}, u32[]{:S(2)}, u32[]{:S(2)}) %collective-permute-start.41) | collective-permute-done | bytes 786464 | tf_op jit(solution)/shard_map/ppermute | solution.py:28
  312.7 8.7 %weight_grad_second.1 = bf16[768,1792]{1,0:T(8,128)(2,1)} custom-call(s32[4]{0:T(128)S(1)} %pad_add_fusion.c_ref, bf16[3,768,1024]{2,1,0:T(8,128)(2,1)} %get-tuple-element.105.refs_0_, bf16[2,512,768]{2,1,0:T(8,128)(2,1)S(1)} %copy-done.1, bf16[2,512,768]{2,1,0:T(8,128)(2,1)S(1)} %copy-done, bf16[2,512,768]{2,1,0:T(8,128)(2,1)S(1)} %copy-done.2, ...), custom_call_target="tpu_custom_call" | custom-call | flops 3019898880 | bytes 18874368 | tf_op jit(solution)/shard_map/weight_grad_second/pallas_call | solution.py:438
  329.9 25.9 %collective-permute-done.53 = f32[4,768]{1,0:T(4,128)S(1)} collective-permute-done((f32[4,768]{1,0:T(4,128)S(1)}, f32[4,768]{1,0:T(4,128)S(1)}, u32[]{:S(2)}, u32[]{:S(2)}) %collective-permute-start.53) | collective-permute-done | bytes 12320 | tf_op jit(solution)/shard_map/ppermute | solution.py:28
  372.5 5.8 %collective-permute-done.49 = bf16[96,1792]{1,0:T(8,128)(2,1)S(1)} collective-permute-done((bf16[96,1792]{1,0:T(8,128)(2,1)S(1)}, bf16[96,1792]{1,0:T(8,128)(2,1)S(1)}, u32[]{:S(2)}, u32[]{:S(2)}) %collective-permute-start.49) | collective-permute-done | bytes 344096 | tf_op jit(solution)/shard_map/ppermute | solution.py:28
  378.2 8.1 %collective-permute-done.51 = bf16[96,1792]{1,0:T(8,128)(2,1)S(1)} collective-permute-done((bf16[96,1792]{1,0:T(8,128)(2,1)S(1)}, bf16[96,1792]{1,0:T(8,128)(2,1)S(1)}, u32[]{:S(2)}, u32[]{:S(2)}) %collective-permute-start.51) | collective-permute-done | bytes 344096 | tf_op jit(solution)/shard_map/ppermute | solution.py:28
  386.3 13.0 %collective-permute-done.50 = bf16[96,1792]{1,0:T(8,128)(2,1)S(1)} collective-permute-done((bf16[96,1792]{1,0:T(8,128)(2,1)S(1)}, bf16[96,1792]{1,0:T(8,128)(2,1)S(1)}, u32[]{:S(2)}, u32[]{:S(2)}) %collective-permute-start.50) | collective-permute-done | bytes 344096 | tf_op jit(solution)/shard_map/ppermute | solution.py:28
  (257 shorter events, 127.6 us)
Async XLA Ops:
  26.4 21.2 %collective-permute-start.13 = (bf16[96,768]{1,0:T(8,128)(2,1)S(1)}, bf16[96,768]{1,0:T(8,128)(2,1)S(1)}, u32[]{:S(2)}, u32[]{:S(2)}) collective-permute-start(bf16[96,768]{1,0:T(8,128)(2,1)S(1)} %convert_element_type.94), channel_id=1, source_target_pairs={{0,16},{4,20},{8,24},{12,28},{16,0},{20,4},{24,8},{28,12},{1,17},{... | collective-permute-start | bytes 442376 | tf_op jit(solution)/shard_map/ppermute | solution.py:28
  27.0 30.4 %collective-permute-start.3 = (bf16[4,112,576]{2,1,0:T(8,128)(2,1)S(1)}, bf16[4,112,576]{2,1,0:T(8,128)(2,1)S(1)}, u32[]{:S(2)}, u32[]{:S(2)}) collective-permute-start(bf16[4,112,576]{2,1,0:T(8,128)(2,1)S(1)} %pad_maximum_fusion.4.refs_0_), channel_id=1, source_target_pairs={{0,4},{4,0},{8,12},{12,8},{16,20},{20,16},{24,28},{28,24},{1,5},{5... | collective-permute-start | bytes 1548296 | tf_op jit(solution)/shard_map/ppermute | solution.py:28
  50.0 42.4 %collective-permute-start.9 = (bf16[4,96,256]{2,1,0:T(8,128)(2,1)S(1)}, bf16[4,96,256]{2,1,0:T(8,128)(2,1)S(1)}, u32[]{:S(2)}, u32[]{:S(2)}) collective-permute-start(bf16[4,96,256]{2,1,0:T(8,128)(2,1)S(1)} %pad_maximum_fusion.7.refs_0_), channel_id=1, source_target_pairs={{0,1},{1,0},{2,3},{3,2},{4,5},{5,4},{6,7},{7,6},{8,9},{9,8},{10,11... | collective-permute-start | bytes 589832 | tf_op jit(solution)/shard_map/ppermute | solution.py:28
  53.3 47.5 %collective-permute-start.20 = (bf16[4,96,768]{2,1,0:T(8,128)(2,1)S(1)}, bf16[4,96,768]{2,1,0:T(8,128)(2,1)S(1)}, u32[]{:S(2)}, u32[]{:S(2)}) collective-permute-start(bf16[4,96,768]{2,1,0:T(8,128)(2,1)S(1)} %pad_maximum_fusion.2.refs_0_), channel_id=1, source_target_pairs={{0,1},{1,0},{2,3},{3,2},{4,5},{5,4},{6,7},{7,6},{8,9},{9,8},{10,11... | collective-permute-start | bytes 1769480 | tf_op jit(solution)/shard_map/ppermute | solution.py:28
  55.2 42.8 %collective-permute-start.15 = (bf16[4,96,768]{2,1,0:T(8,128)(2,1)S(1)}, bf16[4,96,768]{2,1,0:T(8,128)(2,1)S(1)}, u32[]{:S(2)}, u32[]{:S(2)}) collective-permute-start(bf16[4,96,768]{2,1,0:T(8,128)(2,1)S(1)} %pad_maximum_fusion.2.refs_0_), channel_id=1, source_target_pairs={{0,4},{4,0},{8,12},{12,8},{16,20},{20,16},{24,28},{28,24},{1,5},{5... | collective-permute-start | bytes 1769480 | tf_op jit(solution)/shard_map/ppermute | solution.py:28
  56.9 41.6 %collective-permute-start.19 = (bf16[4,96,768]{2,1,0:T(8,128)(2,1)S(1)}, bf16[4,96,768]{2,1,0:T(8,128)(2,1)S(1)}, u32[]{:S(2)}, u32[]{:S(2)}) collective-permute-start(bf16[4,96,768]{2,1,0:T(8,128)(2,1)S(1)} %pad_maximum_fusion.3.refs_2_), channel_id=1, source_target_pairs={{0,4},{4,0},{8,12},{12,8},{16,20},{20,16},{24,28},{28,24},{1,5},{5... | collective-permute-start | bytes 1769480 | tf_op jit(solution)/shard_map/ppermute | solution.py:28
  57.4 35.7 %collective-permute-start.10 = (bf16[4,96,256]{2,1,0:T(8,128)(2,1)S(1)}, bf16[4,96,256]{2,1,0:T(8,128)(2,1)S(1)}, u32[]{:S(2)}, u32[]{:S(2)}) collective-permute-start(bf16[4,96,256]{2,1,0:T(8,128)(2,1)S(1)} %collective-permute-done.8.refs_1_), channel_id=1, source_target_pairs={{0,1},{1,0},{2,3},{3,2},{4,5},{5,4},{6,7},{7,6},{8,9},{9,8},{10,11... | collective-permute-start | bytes 589832 | tf_op jit(solution)/shard_map/ppermute | solution.py:28
  100.8 36.8 %collective-permute-start.11 = (bf16[768,512]{1,0:T(8,128)(2,1)S(1)}, bf16[768,512]{1,0:T(8,128)(2,1)S(1)}, u32[]{:S(2)}, u32[]{:S(2)}) collective-permute-start(bf16[768,512]{1,0:T(8,128)(2,1)S(1)} %out_product.2.own_ref), channel_id=1, source_target_pairs={{0,2},{1,3},{2,0},{3,1},{4,6},{5,7},{6,4},{7,5},{8,10},{9,11},{10,... | collective-permute-start | bytes 2359304 | tf_op jit(solution)/shard_map/ppermute | solution.py:28
  136.1 23.6 %collective-permute-start.32 = (bf16[512,768]{1,0:T(8,128)(2,1)}, bf16[512,768]{1,0:T(8,128)(2,1)S(1)}, u32[]{:S(2)}, u32[]{:S(2)}) collective-permute-start(bf16[512,768]{1,0:T(8,128)(2,1)} %get-tuple-element.71.own_ref), channel_id=1, source_target_pairs={{0,2},{1,3},{2,0},{3,1},{4,6},{5,7},{6,4},{7,5},{8,10},{9,11},{10,... | collective-permute-start | bytes 2359304 | tf_op jit(solution)/shard_map/ppermute | solution.py:28
  157.2 20.8 %collective-permute-start.30 = (bf16[512,768]{1,0:T(8,128)(2,1)}, bf16[512,768]{1,0:T(8,128)(2,1)}, u32[]{:S(2)}, u32[]{:S(2)}) collective-permute-start(bf16[512,768]{1,0:T(8,128)(2,1)} %get-tuple-element.79.own_ref), channel_id=1, source_target_pairs={{0,2},{1,3},{2,0},{3,1},{4,6},{5,7},{6,4},{7,5},{8,10},{9,11},{10,... | collective-permute-start | bytes 2359304 | tf_op jit(solution)/shard_map/ppermute | solution.py:28
  157.7 99.5 %collective-permute-start.37 = (bf16[4,112,576]{2,1,0:T(8,128)(2,1)}, bf16[4,112,576]{2,1,0:T(8,128)(2,1)S(1)}, u32[]{:S(2)}, u32[]{:S(2)}) collective-permute-start(bf16[4,112,576]{2,1,0:T(8,128)(2,1)} %copy-done.17), channel_id=1, source_target_pairs={{0,1},{1,0},{2,3},{3,2},{4,5},{5,4},{6,7},{7,6},{8,9},{9,8},{10,11... | collective-permute-start | bytes 1548296 | tf_op jit(solution)/shard_map/ppermute | solution.py:28
  157.7 99.6 %collective-permute-start.38 = (bf16[4,112,576]{2,1,0:T(8,128)(2,1)}, bf16[4,112,576]{2,1,0:T(8,128)(2,1)S(1)}, u32[]{:S(2)}, u32[]{:S(2)}) collective-permute-start(bf16[4,112,576]{2,1,0:T(8,128)(2,1)} %copy-done.23), channel_id=1, source_target_pairs={{0,1},{1,0},{2,3},{3,2},{4,5},{5,4},{6,7},{7,6},{8,9},{9,8},{10,11... | collective-permute-start | bytes 1548296 | tf_op jit(solution)/shard_map/ppermute | solution.py:28
  158.2 37.9 %collective-permute-start.28 = (bf16[512,768]{1,0:T(8,128)(2,1)}, bf16[512,768]{1,0:T(8,128)(2,1)S(1)}, u32[]{:S(2)}, u32[]{:S(2)}) collective-permute-start(bf16[512,768]{1,0:T(8,128)(2,1)} %get-tuple-element.75), channel_id=1, source_target_pairs={{0,2},{1,3},{2,0},{3,1},{4,6},{5,7},{6,4},{7,5},{8,10},{9,11},{10,... | collective-permute-start | bytes 2359304 | tf_op jit(solution)/shard_map/ppermute | solution.py:28
  169.5 28.3 %collective-permute-start.33 = (bf16[192,512]{1,0:T(8,128)(2,1)S(1)}, bf16[192,512]{1,0:T(8,128)(2,1)S(1)}, u32[]{:S(2)}, u32[]{:S(2)}) collective-permute-start(bf16[192,512]{1,0:T(8,128)(2,1)S(1)} %get-tuple-element.138), channel_id=1, source_target_pairs={{0,1},{1,0},{2,3},{3,2},{4,5},{5,4},{6,7},{7,6},{8,9},{9,8},{10,11... | collective-permute-start | bytes 589832 | tf_op jit(solution)/shard_map/ppermute | solution.py:28
  196.1 116.6 %collective-permute-start.47 = (bf16[768,1792]{1,0:T(8,128)(2,1)}, bf16[768,1792]{1,0:T(8,128)(2,1)}, u32[]{:S(2)}, u32[]{:S(2)}) collective-permute-start(bf16[768,1792]{1,0:T(8,128)(2,1)} %get-tuple-element.106), channel_id=1, source_target_pairs={{0,1},{1,0},{2,3},{3,2},{4,5},{5,4},{6,7},{7,6},{8,9},{9,8},{10,11... | collective-permute-start | bytes 8257544 | tf_op jit(solution)/shard_map/ppermute | solution.py:28
  258.7 22.0 %collective-permute-start.44 = (bf16[96,576]{1,0:T(8,128)(2,1)S(1)}, bf16[96,576]{1,0:T(8,128)(2,1)S(1)}, u32[]{:S(2)}, u32[]{:S(2)}) collective-permute-start(bf16[96,576]{1,0:T(8,128)(2,1)S(1)} %get-tuple-element.134), channel_id=1, source_target_pairs={{0,8},{4,12},{8,0},{12,4},{16,24},{20,28},{24,16},{28,20},{1,9},{5... | collective-permute-start | bytes 331784 | tf_op jit(solution)/shard_map/ppermute | solution.py:28
  266.5 27.5 %collective-permute-start.39 = (bf16[768,512]{1,0:T(8,128)(2,1)}, bf16[768,512]{1,0:T(8,128)(2,1)}, u32[]{:S(2)}, u32[]{:S(2)}) collective-permute-start(bf16[768,512]{1,0:T(8,128)(2,1)} %get-tuple-element.88.own_ref), channel_id=1, source_target_pairs={{0,2},{1,3},{2,0},{3,1},{4,6},{5,7},{6,4},{7,5},{8,10},{9,11},{10,... | collective-permute-start | bytes 2359304 | tf_op jit(solution)/shard_map/ppermute | solution.py:28
  268.1 40.9 %collective-permute-start.41 = (bf16[768,512]{1,0:T(8,128)(2,1)S(1)}, bf16[768,512]{1,0:T(8,128)(2,1)}, u32[]{:S(2)}, u32[]{:S(2)}) collective-permute-start(bf16[768,512]{1,0:T(8,128)(2,1)S(1)} %get-tuple-element.91.own_ref), channel_id=1, source_target_pairs={{0,2},{1,3},{2,0},{3,1},{4,6},{5,7},{6,4},{7,5},{8,10},{9,11},{10,... | collective-permute-start | bytes 2359304 | tf_op jit(solution)/shard_map/ppermute | solution.py:28
  284.9 39.7 %collective-permute-start.29 = (bf16[512,768]{1,0:T(8,128)(2,1)}, bf16[512,768]{1,0:T(8,128)(2,1)}, u32[]{:S(2)}, u32[]{:S(2)}) collective-permute-start(bf16[512,768]{1,0:T(8,128)(2,1)} %add_convert_fusion.1), channel_id=1, source_target_pairs={{0,1},{1,0},{2,3},{3,2},{4,5},{5,4},{6,7},{7,6},{8,9},{9,8},{10,11... | collective-permute-start | bytes 2359304 | tf_op jit(solution)/shard_map/ppermute | solution.py:28
  288.2 39.4 %collective-permute-start.27 = (bf16[512,768]{1,0:T(8,128)(2,1)}, bf16[512,768]{1,0:T(8,128)(2,1)}, u32[]{:S(2)}, u32[]{:S(2)}) collective-permute-start(bf16[512,768]{1,0:T(8,128)(2,1)} %add_convert_fusion.2), channel_id=1, source_target_pairs={{0,1},{1,0},{2,3},{3,2},{4,5},{5,4},{6,7},{7,6},{8,9},{9,8},{10,11... | collective-permute-start | bytes 2359304 | tf_op jit(solution)/shard_map/ppermute | solution.py:28
  322.9 41.9 %collective-permute-start.48 = (bf16[384,1792]{1,0:T(8,128)(2,1)S(1)}, bf16[384,1792]{1,0:T(8,128)(2,1)S(1)}, u32[]{:S(2)}, u32[]{:S(2)}) collective-permute-start(bf16[384,1792]{1,0:T(8,128)(2,1)S(1)} %slice.146), channel_id=1, source_target_pairs={{0,4},{4,0},{8,12},{12,8},{16,20},{20,16},{24,28},{28,24},{1,5},{5... | collective-permute-start | bytes 4128776 | tf_op jit(solution)/shard_map/ppermute | solution.py:28
  326.8 37.4 %collective-permute-start.40 = (bf16[512,768]{1,0:T(8,128)(2,1)S(1)}, bf16[512,768]{1,0:T(8,128)(2,1)S(1)}, u32[]{:S(2)}, u32[]{:S(2)}) collective-permute-start(bf16[512,768]{1,0:T(8,128)(2,1)S(1)} %get-tuple-element.90), channel_id=1, source_target_pairs={{0,1},{1,0},{2,3},{3,2},{4,5},{5,4},{6,7},{7,6},{8,9},{9,8},{10,11... | collective-permute-start | bytes 2359304 | tf_op jit(solution)/shard_map/ppermute | solution.py:28
  327.1 28.7 %collective-permute-start.53 = (f32[4,768]{1,0:T(4,128)S(1)}, f32[4,768]{1,0:T(4,128)S(1)}, u32[]{:S(2)}, u32[]{:S(2)}) collective-permute-start(f32[4,768]{1,0:T(4,128)S(1)} %fusion.3), channel_id=1, source_target_pairs={{0,4},{4,0},{8,12},{12,8},{16,20},{20,16},{24,28},{28,24},{1,5},{5... | collective-permute-start | bytes 36872 | tf_op jit(solution)/shard_map/ppermute | solution.py:28
  369.9 29.4 %collective-permute-start.50 = (bf16[96,1792]{1,0:T(8,128)(2,1)S(1)}, bf16[96,1792]{1,0:T(8,128)(2,1)S(1)}, u32[]{:S(2)}, u32[]{:S(2)}) collective-permute-start(bf16[96,1792]{1,0:T(8,128)(2,1)S(1)} %get-tuple-element.131), channel_id=1, source_target_pairs={{0,16},{4,20},{8,24},{12,28},{16,0},{20,4},{24,8},{28,12},{1,17},{... | collective-permute-start | bytes 1032200 | tf_op jit(solution)/shard_map/ppermute | solution.py:28
  (79 other events, 823.7 us)
